TPU v7x, 128 devices: a whole 4x4x4 slice. The times are simulated.
128 devices in a mesh: row: 8 (over z_hi, y), col: 16 (over z_lo, x, core).
Axes of the slice: x: 4, y: 4, z: 4 (z_hi: 2, z_lo: 2; z = z_hi * 2 + z_lo), core: 2. Of those that a mesh axis runs over, the one named last changes fastest.
Arguments:
- features: float32 [2, 131072, 256], P(None, ('row', 'col')), may hold values from -7 to 7
- adj_vals: bfloat16 [2, 1024, 20, 128, 128], P(None, ('row', 'col')), may hold values from 0.049804688 to 1
- blk_cols: int32 [2, 1024, 20], P(None, ('row', 'col')), may hold values from 0 to 11
- blk_count: int32 [2, 1024], P(None, ('row', 'col')), may hold values from 1 to 20
- send_list: int32 [2, 128, 512], P(None, ('row', 'col')), may hold values from 0 to 1023
- weight: float32 [256, 256], replicated, may hold values from -0.375 to 0.375
- cand_tiles: int32 [8, 16, 2, 48], P('row', 'col'), may hold values from 0 to 127, as said below
- cand_count: int32 [8, 16], P('row', 'col'), may hold values from 8 to 48, as said below
Outputs:
- log_plan: float32 [8, 16, 48, 128, 128], P('row', 'col')
- row_potential: float32 [8, 16, 1024], P('row')
- col_potential: float32 [8, 16, 1024], P(None, 'col')
Inputs may be any that keep to these rules, and one draw needn't show every extreme that they name: Blocks at or past blk_count are padding. send_list[g, q, p * 4 + i] is the i-th own row that partition q sends to partition p. `cand_tiles`: every slot, live or not, holds a valid pair; no live pair repeats on one device; every tile of every source group and of every target group lies in some live slot; for each device and each partition of its row, at most 3 of the device's 48 slots name source tiles of that partition, and on every device some partition has exactly 3. `cand_count`: some device has all 48 slots live.
All inputs are finite; a program needn't handle non-finite values.
Results may differ from a plain program's by a relative error of at most 0.0003.
Values sent between devices are 32-bit elements; how exact they have to be, the bound alone decides.
A program may use at most 128 MiB of HBM per device.

v0:
```python
import math

import jax
import jax.numpy as jnp
from jax import lax
from jax.sharding import Mesh
from jax.sharding import PartitionSpec as P

TILE = 128
TD = 8
CAP = 48
ITERS = 2
COL = ("col_0", "col_1", "col_2")
ROW_COL = ("row", "col_0", "col_1", "col_2")


HIGHEST = lax.Precision.HIGHEST
SHARPNESS = 2.0
NEGATIVE = -1e30


def joined_all(array, axes, combine):
    for axis in axes:
        pieces = jax.tree.map(lambda part: lax.all_gather(part, axis), array)
        array = jax.tree.map(lambda part: part[0], pieces)
        for k in range(1, lax.axis_size(axis)):
            array = combine(array, jax.tree.map(lambda part: part[k], pieces))
    return array


def from_everyone(array, axis):
    size = lax.axis_size(axis)
    return lax.all_to_all(
        jnp.broadcast_to(array[None], (size, *array.shape)), axis, 0, 0, tiled=True
    )


def gathered_once(array, axis):
    leaves = jax.tree.leaves(array)
    turns = sorted(range(len(leaves)), key=lambda k: -leaves[k].size)
    width = (1, *leaves[turns[0]].shape)[-1]
    lines = [
        jnp.pad(leaves[k].reshape(-1), (0, -leaves[k].size % width)).reshape(-1, width)
        for k in turns
    ]
    both, at, found = (from_everyone(jnp.concatenate(lines), axis), 0, {})
    for k, line in zip(turns, lines):
        share = both[:, at : at + len(line)].reshape(len(both), -1)
        found[k] = share[:, : leaves[k].size].reshape(-1, *leaves[k].shape)
        at += len(line)
    numbers = iter(range(len(leaves)))
    return jax.tree.map(lambda _: found[next(numbers)], array)


def gathered_by_type(array, axis):
    leaves, found = (jax.tree.leaves(array), {})
    for leading, a in enumerate(leaves):
        if leading not in found:
            alike = [k for k, b in enumerate(leaves) if b.dtype == a.dtype]
            got = (
                gathered_once([leaves[k] for k in alike], axis)
                if len(alike) > 1
                else [from_everyone(a, axis)]
            )
            for k, b in zip(alike, got):
                found[k] = b
    numbers = iter(range(len(leaves)))
    return jax.tree.map(lambda _: found[next(numbers)], array)


def joined_by_halves(pieces, combine):
    while len(jax.tree.leaves(pieces)[0]) > 1:
        pieces = jax.vmap(combine)(
            *(jax.tree.map(lambda part: part[side::2], pieces) for side in (0, 1))
        )
    return jax.tree.map(lambda part: part[0], pieces)


def combined_all(array, axis, combine):
    pieces = gathered_by_type(array, axis)
    return joined_by_halves(pieces, combine)


def aggregate(lookup, block_vals, block_cols, block_count, weight, own_rows):
    num_tiles = block_vals.shape[0]
    listed = (jnp.arange(block_vals.shape[1])[None, :] < block_count[:, None]).astype(jnp.float32)

    def add_block(state_pair, block_index):
        summed, degree = state_pair
        weights_now = (
            block_vals[:, block_index].astype(jnp.float32) * listed[:, block_index][:, None, None]
        )
        picked = lookup[block_cols[:, block_index]]
        summed = summed + jnp.einsum("tij,tjd->tid", weights_now, picked, precision=HIGHEST)
        degree = degree + jnp.sum(weights_now, axis=2)
        return ((summed, degree), None)

    start_sum = jnp.zeros((num_tiles, TILE, lookup.shape[2]), jnp.float32)
    start_deg = jnp.zeros((num_tiles, TILE), jnp.float32)
    (summed, degree), unused = lax.scan(
        add_block, (start_sum, start_deg), jnp.arange(block_vals.shape[1])
    )
    mixed_rows = (summed / jnp.sqrt(degree)[:, :, None]).reshape(num_tiles * TILE, -1)
    return own_rows + jax.nn.relu(jnp.dot(mixed_rows, weight, precision=HIGHEST))


def pick_rows(source_rows, picked_rows):
    return source_rows[picked_rows]


def combine_lse(first_pair, second_pair):
    larger = jnp.maximum(first_pair[0], second_pair[0])
    merged_sum = first_pair[1] * jnp.exp(first_pair[0] - larger) + second_pair[1] * jnp.exp(
        second_pair[0] - larger
    )
    return (larger, merged_sum)


def lookup_rows(one_hot, table_values):
    return jnp.dot(one_hot, table_values, precision=HIGHEST)


def row_potential_of(values, grouped, picker, live_float):
    slot_max = jnp.max(values, axis=2)
    group_max = jnp.max(jnp.where(grouped[:, :, None], slot_max[:, None, :], NEGATIVE), axis=0)
    shift_back = lookup_rows(picker, group_max)
    slot_sums = jnp.sum(jnp.exp(values - shift_back[:, :, None]), axis=2)
    group_sum = jnp.einsum("sr,sc->rc", live_float, slot_sums, precision=HIGHEST)
    group_max, group_sum = joined_all((group_max, group_sum), COL, combine_lse)
    return -(group_max + jnp.log(group_sum))


def col_potential_of(values, grouped, picker, live_float):
    slot_max = jnp.max(values, axis=1)
    group_max = jnp.max(jnp.where(grouped[:, :, None], slot_max[:, None, :], NEGATIVE), axis=0)
    shift_back = lookup_rows(picker, group_max)
    slot_sums = jnp.sum(jnp.exp(values - shift_back[:, None, :]), axis=1)
    group_sum = jnp.einsum("sr,sc->rc", live_float, slot_sums, precision=HIGHEST)
    group_max, group_sum = combined_all((group_max, group_sum), "row", combine_lse)
    return -(group_max + jnp.log(group_sum))


def on_device(features, adj_vals, blk_cols, blk_count, send_list, weight, cand_tiles, cand_count):
    feat_width = features.shape[2]
    outgoing = jax.vmap(pick_rows)(features, send_list[:, 0])
    ghost_rows = lax.all_to_all(outgoing, ROW_COL, split_axis=1, concat_axis=1, tiled=True)
    embedded = []
    for graph_id in range(2):
        lookup = jnp.concatenate([features[graph_id], ghost_rows[graph_id]], axis=0).reshape(
            -1, TILE, feat_width
        )
        embedded.append(
            aggregate(
                lookup,
                adj_vals[graph_id],
                blk_cols[graph_id],
                blk_count[graph_id],
                weight,
                features[graph_id],
            )
        )
    source_embed = embedded[0]
    target_embed = embedded[1]
    row_count = lax.axis_size("row")
    col_count = lax.axis_size(COL)
    rows_here = cand_tiles[0, 0, 0]
    cols_here = cand_tiles[0, 0, 1]
    slot_index = jnp.arange(CAP, dtype=jnp.int32)
    slot_live = slot_index < cand_count[0, 0]
    target_group = lax.all_gather(target_embed, "row", axis=0, tiled=True).reshape(
        -1, TILE, feat_width
    )
    target_tiles = target_group[cols_here]
    source_group = lax.all_gather(source_embed, COL, axis=0, tiled=True).reshape(
        -1, TILE, feat_width
    )
    source_tiles = source_group[rows_here]
    logits = (
        SHARPNESS
        / math.sqrt(feat_width)
        * jnp.einsum("sid,sjd->sij", source_tiles, target_tiles, precision=HIGHEST)
    )
    row_onehot = rows_here[:, None] == jnp.arange(TD * col_count, dtype=jnp.int32)[None, :]
    col_onehot = cols_here[:, None] == jnp.arange(TD * row_count, dtype=jnp.int32)[None, :]
    row_grouped = row_onehot & slot_live[:, None]
    col_grouped = col_onehot & slot_live[:, None]
    row_picker = row_onehot.astype(jnp.float32)
    col_picker = col_onehot.astype(jnp.float32)
    row_livef = row_grouped.astype(jnp.float32)
    col_livef = col_grouped.astype(jnp.float32)
    live_cube = slot_live[:, None, None]
    col_pot = jnp.zeros((TD * row_count, TILE), jnp.float32)
    row_pot = jnp.zeros((TD * col_count, TILE), jnp.float32)
    for sweep_id in range(ITERS):
        col_slot = lookup_rows(col_picker, col_pot)
        values = jnp.where(live_cube, logits + col_slot[:, None, :], NEGATIVE)
        row_pot = row_potential_of(values, row_grouped, row_picker, row_livef)
        row_slot = lookup_rows(row_picker, row_pot)
        values = jnp.where(live_cube, logits + row_slot[:, :, None], NEGATIVE)
        col_pot = col_potential_of(values, col_grouped, col_picker, col_livef)
    row_slot = lookup_rows(row_picker, row_pot)
    col_slot = lookup_rows(col_picker, col_pot)
    log_plan = jnp.where(live_cube, logits + row_slot[:, :, None] + col_slot[:, None, :], 0.0)
    return (
        log_plan[None, None],
        row_pot.reshape(1, col_count, -1),
        col_pot.reshape(row_count, 1, -1),
    )


def solution(mesh):
    finer = Mesh(
        mesh.devices.reshape(mesh.shape["row"], 2, 4, 2), ("row", "col_0", "col_1", "col_2")
    )
    placed = (
        P(None, ROW_COL, None),
        P(None, ROW_COL, None, None, None),
        P(None, ROW_COL, None),
        P(None, ROW_COL),
        P(None, ROW_COL, None),
        P(),
        P("row", COL, None, None),
        P("row", COL),
    )
    return jax.shard_map(
        on_device,
        mesh=finer,
        in_specs=placed,
        out_specs=(P("row", COL, None, None, None), P("row", None, None), P(None, COL, None)),
        check_vma=False,
    )
```

profile of v0, /device:TPU:0, one launch (start us, length us, event | category | flops | bytes accessed | tf_op | source)
XLA Modules:
  0.0 696.8 jit_solution(7761243411783571190)
XLA Ops:
  7.9 12.6 %gather_fusion.4 = f32[1024,256]{1,0:T(8,128)S(1)} fusion(f32[2,1024,256]{2,1,0:T(8,128)} %param.12, s32[1024]{0:T(1024)S(1)} %bitcast.240), kind=kCustom, calls=%fused_computation.4 | custom fusion | bytes 2105344 | tf_op jit(solution)/shard_map/vmap()/gather | solution.py:108
  22.4 11.1 %all-to-all-start = ((f32[2,512,256]{2,0,1:T(2,128)}), f32[2,512,256]{2,0,1:T(2,128)S(1)}, u32[]{:S(2)}, u32[]{:S(2)}) async-start(f32[2,512,256]{2,0,1:T(2,128)} %copy.24), calls=%async_computation | async-start | bytes 2097152 | tf_op jit(solution)/shard_map/all_to_all | solution.py:146
  33.6 12.8 %fusion.125 = (bf16[1,8,20,128,128]{4,3,2,1,0:T(8,128)(2,1)}, bf16[1,8,20,128,128]{4,3,2,1,0:T(8,128)(2,1)}) fusion(bf16[2,8,20,128,128]{4,3,2,1,0:T(8,128)(2,1)} %param.13), kind=kLoop, calls=%fused_computation.219 | loop fusion | bytes 20971520 | tf_op jit(solution)/shard_map/slice | solution.py:155
  48.2 12.7 %copy_bitcast_fusion = (bf16[8,20,128,128]{3,2,0,1:T(8,128)(2,1)}, bf16[8,20,128,128]{3,2,0,1:T(8,128)(2,1)}) fusion(bf16[1,8,20,128,128]{4,3,2,1,0:T(8,128)(2,1)} %get-tuple-element.195, bf16[1,8,20,128,128]{4,3,2,1,0:T(8,128)(2,1)} %get-tuple-element.196), kind=kLoop, calls=%fused_computation.33 | loop fusion | bytes 20971520 | tf_op jit(solution)/shard_map/squeeze | solution.py:155
  63.9 180.3 %while.27 = (s32[]{:T(128)}, f32[8,128,256]{2,1,0:T(8,128)}, f32[8,128]{1,0:T(8,128)S(1)}, s32[20]{0:T(128)S(1)}, bf16[8,20,128,128]{3,2,0,1:T(8,128)(2,1)}, /*i...) while((s32[]{:T(128)}, f32[8,128,256]{2,1,0:T(8,128)}, ...), condition=%wide.region_5.6_spmd.clone, body=%wide.region_3.5_spmd.clone.sunk | while | flops 403834912 | bytes 5788086 | solution.py:100
  250.3 186.5 %while.26 = (s32[]{:T(128)}, f32[8,128,256]{2,1,0:T(8,128)}, f32[8,128]{1,0:T(8,128)S(1)}, s32[20]{0:T(128)S(1)}, bf16[8,20,128,128]{3,2,0,1:T(8,128)(2,1)}, /*i...) while((s32[]{:T(128)}, f32[8,128,256]{2,1,0:T(8,128)}, ...), condition=%wide.region_2.3_spmd.clone, body=%wide.region_0.2_spmd.clone.sunk | while | flops 403834912 | bytes 5788086 | solution.py:100
  263.9 3.5 convolution_add_fusion.4
  273.2 3.5 convolution_add_fusion.4
  282.6 3.5 convolution_add_fusion.4
  291.9 3.6 convolution_add_fusion.4
  320.1 3.5 convolution_add_fusion.4
  329.4 3.5 convolution_add_fusion.4
  338.8 3.5 convolution_add_fusion.4
  348.1 3.5 convolution_add_fusion.4
  357.4 3.5 convolution_add_fusion.4
  404.1 3.5 convolution_add_fusion.4
  432.1 3.5 convolution_add_fusion.4
  441.3 7.0 %gather_fusion.3 = f32[48,128,256]{2,1,0:T(8,128)} fusion(f32[64,128,256]{2,1,0:T(8,128)} %bitcast.243, s32[1024]{0:T(1024)S(1)} %get-tuple-element.225), kind=kCustom, calls=%fused_computation.3 | custom fusion | bytes 12583104 | tf_op jit(solution)/shard_map/gather | solution.py:173
  448.4 84.8 %all-gather.7.cloned.1.call-done = f32[16384,256]{1,0:T(8,128)} async-done(((f32[1024,256]{1,0:T(8,128)}), f32[16384,256]{1,0:T(8,128)}) %all-gather.7.cloned.1.call-update) | async-done | bytes 16777232 | tf_op jit(solution)/shard_map/all_gather | solution.py:174
  533.2 9.4 %gather_fusion.2 = f32[48,128,256]{2,1,0:T(8,128)} fusion(f32[128,128,256]{2,1,0:T(8,128)} %bitcast.247, s32[1024]{0:T(1024)S(1)} %get-tuple-element.226), kind=kCustom, calls=%fused_computation.2 | custom fusion | bytes 12583104 | tf_op jit(solution)/shard_map/gather | solution.py:177
  542.6 9.2 %fusion.14 = (f32[48,128]{1,0:T(8,128)S(1)}, f32[48,128,128]{2,1,0:T(8,128)S(1)}) fusion(f32[48,128]{1,0:T(8,128)S(1)} %fusion.88, pred[48]{0:T(512)(128)(4,1)S(1)} %iota_compare_fusion.13, f32[48,128,256]{2,1,0:T(8,128)} %gather_fusion.2, f32[48,128,256]{2,1,0:T(8,128)} %gather_fusion.3), kind=kOutput, calls=%fused_computation.46 | convolution fusion | flops 2419058688 | bytes 15777840 | tf_op jit(solution)/shard_map/sid,sjd->sij/dot_general | solution.py:181
  553.2 4.9 all-gather
  560.6 4.9 all-gather.1
  565.6 12.6 %all_gather.66 = f32[4,128,128]{2,1,0:T(8,128)S(1)} all-gather(f32[1,128,128]{2,1,0:T(8,128)S(1)} %get-tuple-element.194), channel_id=1, replica_groups=mesh['row'=8,'col_0'=2,'col_1'=4,'col_2'=2] {'col_1'}, dimensions={0}, use_global_device_ids=true | all-gather | bytes 327680 | tf_op jit(solution)/shard_map/all_gather | solution.py:24
  578.2 12.2 %all_gather.70 = f32[4,128,128]{2,1,0:T(8,128)S(1)} all-gather(f32[1,128,128]{2,1,0:T(8,128)S(1)} %get-tuple-element.193), channel_id=1, replica_groups=mesh['row'=8,'col_0'=2,'col_1'=4,'col_2'=2] {'col_1'}, dimensions={0}, use_global_device_ids=true | all-gather | bytes 327680 | tf_op jit(solution)/shard_map/all_gather | solution.py:24
  598.2 18.3 %all_to_all.15 = f32[8,128,128]{2,1,0:T(8,128)S(1)} all-to-all(f32[8,128,128]{2,1,0:T(8,128)S(1)} %broadcast_in_dim.144), channel_id=1, replica_groups=mesh['row'=8,'col_0'=2,'col_1'=4,'col_2'=2] {'row'}, dimensions={0} | all-to-all | bytes 1048576 | tf_op jit(solution)/shard_map/all_to_all | solution.py:33
  619.5 4.9 all-gather.2
  626.9 4.9 all-gather.3
  631.9 12.3 %all_gather.74 = f32[4,128,128]{2,1,0:T(8,128)S(1)} all-gather(f32[1,128,128]{2,1,0:T(8,128)S(1)} %get-tuple-element.186), channel_id=1, replica_groups=mesh['row'=8,'col_0'=2,'col_1'=4,'col_2'=2] {'col_1'}, dimensions={0}, use_global_device_ids=true | all-gather | bytes 327680 | tf_op jit(solution)/shard_map/all_gather | solution.py:24
  644.2 12.2 %all_gather.78 = f32[4,128,128]{2,1,0:T(8,128)S(1)} all-gather(f32[1,128,128]{2,1,0:T(8,128)S(1)} %get-tuple-element.185), channel_id=1, replica_groups=mesh['row'=8,'col_0'=2,'col_1'=4,'col_2'=2] {'col_1'}, dimensions={0}, use_global_device_ids=true | all-gather | bytes 327680 | tf_op jit(solution)/shard_map/all_gather | solution.py:24
  669.2 4.2 all-to-all-start.2
  677.3 8.3 %all-to-all-done.2 = f32[8,128,128]{2,1,0:T(8,128)} async-done(((f32[8,128,128]{2,1,0:T(8,128)}), f32[8,128,128]{2,1,0:T(8,128)}, u32[]{:S(2)}, u32[]{:S(2)}) %all-to-all-start.2) | async-done | bytes 524320 | tf_op jit(solution)/shard_map/all_to_all | solution.py:33
  (420 shorter events, 307.9 us)
Async XLA Ops:
  7.2 238.6 %copy-start = (f32[256,256]{1,0:T(8,128)S(1)}, f32[256,256]{1,0:T(8,128)}, u32[]{:S(2)}) copy-start(f32[256,256]{1,0:T(8,128)} %param.17) | copy-start | bytes 786436
  22.4 38.6 %all-to-all-start = ((f32[2,512,256]{2,0,1:T(2,128)}), f32[2,512,256]{2,0,1:T(2,128)S(1)}, u32[]{:S(2)}, u32[]{:S(2)}) async-start(f32[2,512,256]{2,0,1:T(2,128)} %copy.24), calls=%async_computation | async-start | bytes 2097152 | tf_op jit(solution)/shard_map/all_to_all | solution.py:146
  33.5 407.8 %all-gather.9.cloned.1.call-start = ((), (), s32[]{:S(2)}) async-start(), calls=%async_computation.4 | async-start | bytes 9437184 | tf_op jit(solution)/shard_map/all_gather | solution.py:170
  33.6 12.9 %copy-start.11 = (s32[2,8]{1,0:T(2,128)S(1)}, s32[2,8]{1,0:T(2,128)}, u32[]{:S(2)}) copy-start(s32[2,8]{1,0:T(2,128)} %param.15) | copy-start | bytes 196
  33.6 12.9 %copy-start.7 = (s32[2,8,20]{2,1,0:T(8,128)S(1)}, s32[2,8,20]{2,1,0:T(8,128)}, u32[]{:S(2)}) copy-start(s32[2,8,20]{2,1,0:T(8,128)} %param.14) | copy-start | bytes 3844
  33.6 13.0 %copy-start.1 = (f32[2,1024,256]{2,1,0:T(8,128)S(1)}, f32[2,1024,256]{2,1,0:T(8,128)}, u32[]{:S(2)}) copy-start(f32[2,1024,256]{2,1,0:T(8,128)} %param.12) | copy-start | bytes 6291460
  60.9 1.7 copy-start.3
  244.2 3.8 copy-start.2
  247.8 285.4 %all-gather.7.cloned.1.call-start = ((), (), s32[]{:S(2)}) async-start(), calls=%async_computation.3 | async-start | bytes 17825792 | tf_op jit(solution)/shard_map/all_gather | solution.py:174
  436.8 4.1 copy-start.8
  440.9 175.7 %copy-start.9 = (s32[48]{0:T(128)}, s32[48]{0:T(128)S(1)}, u32[]{:S(2)}) copy-start(s32[48]{0:T(128)S(1)} %get-tuple-element.211) | copy-start | bytes 580
  659.0 0.7 copy-start.4
  664.1 4.0 copy-start.5
  664.1 4.0 copy-start.10
  669.2 16.4 %all-to-all-start.2 = ((f32[8,128,128]{2,1,0:T(8,128)}), f32[8,128,128]{2,1,0:T(8,128)}, u32[]{:S(2)}, u32[]{:S(2)}) async-start(f32[8,128,128]{2,1,0:T(8,128)} %broadcast_in_dim.147), calls=%async_computation.2 | async-start | bytes 1048576 | tf_op jit(solution)/shard_map/all_to_all | solution.py:33
  686.8 3.2 copy-start.6
Sparse Core Ops, SparseCore 0:
  247.9 110.0 all-gather.8
  440.3 92.8 all-gather.6
where the time goes:
time: 703 us; the launch traced here: 697 us
  local copies, waits for them, and re-layouts  171 us (24%)
  matrix products  154 us (22%)
  blocking collectives  95.3 us (14%)
  waiting for transfers between devices  93.2 us (13%)
  other arithmetic  77 us (11%)
  loops' own time  75.8 us (11%)
  starting transfers between devices  15.6 us (2%)
  between operations  15.3 us (2%)
    dot_general x40, matrix products, add_block(): jnp.einsum('tij,tjd->tid', weights_now, picked, precision=HIGHEST)  136 us
    all_gather x1, waiting for transfers between devices, on_device(): lax.all_gather(source_embed, COL, axis=0, tiled=True)  84.8 us
    gather x40, local copies, waits for them, and re-layouts, add_block(): picked = lookup[block_cols[:, block_index]]  81 us
    all_gather x12, blocking collectives, joined_all(): pieces = jax.tree.map(lambda part: lax.all_gather(part, axis), array)  76.9 us
    another operation x2, loops' own time, aggregate(): lax.scan(add_block, (start_sum, start_deg), jnp.arange(block_vals.shape[1]))  75.8 us
    reduce_sum x40, other arithmetic, add_block(): degree = degree + jnp.sum(weights_now, axis=2)  48.9 us
    dynamic_slice x40, local copies, waits for them, and re-layouts, aggregate(): lax.scan(add_block, (start_sum, start_deg), jnp.arange(block_vals.shape[1]))  23.6 us
    all_to_all x1, blocking collectives, from_everyone(): lax.all_to_all(jnp.broadcast_to(array[None], (size, *array.shape)), axis,...  18.3 us
  transfers between devices with their start and end apart: 4, of which 2 were waited for; matrix products, arithmetic and copies ran while one was open for 27% of the time, Pallas kernels for 0%

commit v1 on v0

v1 whole, which is shorter than its diff:
```python
import math

import jax
import jax.numpy as jnp
from jax import lax
from jax.experimental import pallas as pl
from jax.experimental.pallas import tpu as pltpu
from jax.sharding import PartitionSpec as P

TILE = 128
TD = 8
CAP = 48
ITERS = 2
HIGH = lax.Precision.HIGH
SHARPNESS = 2.0
NEGATIVE = -1e30
F32 = jnp.float32
BF16 = jnp.bfloat16


def split_two(x):
    hi = x.astype(BF16)
    return hi, (x - hi.astype(F32)).astype(BF16)


def aggregate_kernel(cols, count, adj_ref, own_ref, ghost_ref, weight_ref, out_ref, table, wstack, acc, deg):
    t = pl.program_id(0)
    own_rows, width = own_ref.shape

    @pl.when(t == 0)
    def _():
        for start in range(0, own_rows, 256):
            hi, lo = split_two(own_ref[start : start + 256])
            table[start : start + 256, :width] = hi
            table[start : start + 256, width:] = lo
        for start in range(0, ghost_ref.shape[0], 256):
            hi, lo = split_two(ghost_ref[start : start + 256])
            table[own_rows + start : own_rows + start + 256, :width] = hi
            table[own_rows + start : own_rows + start + 256, width:] = lo
        hi, lo = split_two(weight_ref[...])
        wstack[:width] = hi
        wstack[width : 2 * width] = lo
        wstack[2 * width :] = hi

    acc[...] = jnp.zeros_like(acc)
    deg[...] = jnp.zeros_like(deg)
    n = count[t]

    def pair(i, carry):
        b = 2 * i
        first = adj_ref[0, b]
        second = adj_ref[0, b + 1]
        second = jnp.where(b + 1 < n, second, jnp.zeros_like(second))
        one = table[pl.ds(pl.multiple_of(cols[t, b] * TILE, TILE), TILE), :]
        two = table[pl.ds(pl.multiple_of(cols[t, b + 1] * TILE, TILE), TILE), :]
        left = jnp.concatenate([first, second], axis=1)
        right = jnp.concatenate([one, two], axis=0)
        acc[...] += jnp.dot(left, right, preferred_element_type=F32)
        deg[...] += first.astype(F32) + second.astype(F32)
        return carry

    lax.fori_loop(0, (n + 1) // 2, pair, 0)
    summed = acc[:, :width] + acc[:, width:]
    degree = jnp.sum(deg[...], axis=1, keepdims=True)
    hi, lo = split_two(summed / jnp.sqrt(degree))
    mixed = jnp.dot(jnp.concatenate([hi, hi, lo], axis=1), wstack[...], preferred_element_type=F32)
    own = own_ref[pl.ds(pl.multiple_of(t * TILE, TILE), TILE), :]
    out_ref[...] = own + jnp.maximum(mixed, 0.0)


def aggregate(own, ghost, adj, cols, count, weight, graph):
    rows, width = own.shape[1:]
    tiles, blocks = adj.shape[1:3]
    grid_spec = pltpu.PrefetchScalarGridSpec(
        num_scalar_prefetch=2,
        grid=(tiles,),
        in_specs=[
            pl.BlockSpec((None, 1, blocks, TILE, TILE), lambda t, *_: (graph, t, 0, 0, 0)),
            pl.BlockSpec((None, rows, width), lambda t, *_: (graph, 0, 0)),
            pl.BlockSpec((None, ghost.shape[1], width), lambda t, *_: (graph, 0, 0)),
            pl.BlockSpec((width, width), lambda t, *_: (0, 0)),
        ],
        out_specs=pl.BlockSpec((TILE, width), lambda t, *_: (t, 0)),
        scratch_shapes=[
            pltpu.VMEM((rows + ghost.shape[1], 2 * width), BF16),
            pltpu.VMEM((3 * width, width), BF16),
            pltpu.VMEM((TILE, 2 * width), F32),
            pltpu.VMEM((TILE, TILE), F32),
        ],
    )
    return pl.pallas_call(
        aggregate_kernel,
        grid_spec=grid_spec,
        out_shape=jax.ShapeDtypeStruct((rows, width), F32),
        compiler_params=pltpu.CompilerParams(vmem_limit_bytes=24 * 2**20),
        cost_estimate=pl.CostEstimate(
            flops=tiles * blocks * TILE * TILE * width * 4, bytes_accessed=8 * 2**20, transcendentals=0
        ),
        name="aggregate",
    )(cols[graph], count[graph], adj, own, ghost, weight)


def merged(parts):
    top = jnp.max(parts, axis=0)
    return top + jnp.log(jnp.sum(jnp.exp(parts - top[None]), axis=0))


def tile_lse(slot_lse, grouped):
    spread = jnp.where(grouped[:, :, None], slot_lse[:, None, :], NEGATIVE)
    top = jnp.max(spread, axis=0)
    total = jnp.sum(jnp.where(grouped[:, :, None], jnp.exp(spread - top[None]), 0.0), axis=0)
    return jnp.where(total > 0.0, top + jnp.log(jnp.maximum(total, 1e-30)), NEGATIVE)


def slot_lse(values, axis):
    top = jnp.max(values, axis=axis)
    return top + jnp.log(jnp.sum(jnp.exp(values - jnp.expand_dims(top, axis)), axis=axis))


def everyone(lse, axis):
    size = lax.axis_size(axis)
    mine = lax.all_to_all(lse.reshape(size, TD, TILE), axis, 0, 0, tiled=True)
    return lax.all_gather(-merged(mine), axis, axis=0, tiled=True)


def on_device(features, adj_vals, blk_cols, blk_count, send_list, weight, cand_tiles, cand_count):
    width = features.shape[2]
    row_count = lax.axis_size("row")
    col_count = lax.axis_size("col")
    devices = row_count * col_count
    rows_dev = features.shape[1]

    rows_here = cand_tiles[0, 0, 0]
    cols_here = cand_tiles[0, 0, 1]
    share = CAP // col_count
    wanted = lax.all_gather(rows_here, "col")
    part = wanted // TD
    slots = jnp.arange(CAP, dtype=jnp.int32)
    earlier = slots[None, :] < slots[:, None]
    rank = jnp.sum((part[:, :, None] == part[:, None, :]) & earlier[None], axis=2, dtype=jnp.int32)
    me = lax.axis_index("col")
    hit = (part == me)[:, None, :] & (rank[:, None, :] == jnp.arange(share)[None, :, None])
    asked = jnp.sum(jnp.where(hit, (wanted % TD)[:, None, :], 0), axis=2, dtype=jnp.int32)
    my_part = rows_here // TD
    my_rank = jnp.sum((my_part[:, None] == my_part[None, :]) & earlier, axis=1, dtype=jnp.int32)
    place = jnp.clip(my_part * share + my_rank, 0, CAP - 1)

    picks = send_list[:, 0] + jnp.arange(2, dtype=jnp.int32)[:, None] * rows_dev
    per_dest = send_list.shape[2] // devices
    picks = picks.reshape(2, devices, per_dest).transpose(1, 0, 2).reshape(-1)
    outgoing = features.reshape(2 * rows_dev, width)[picks].reshape(devices, 2 * per_dest, width)
    ghost = lax.all_to_all(outgoing, ("row", "col"), 0, 0, tiled=True)
    ghost = ghost.reshape(devices, 2, per_dest, width).transpose(1, 0, 2, 3).reshape(2, -1, width)

    target = aggregate(features, ghost, adj_vals, blk_cols, blk_count[:, :], weight, 1)
    target_group = lax.all_gather(target, "row", axis=0, tiled=True).reshape(-1, TILE, width)
    source = aggregate(features, ghost, adj_vals, blk_cols, blk_count, weight, 0)
    sent = source.reshape(TD, TILE, width)[asked.reshape(-1)].reshape(col_count, share * TILE, width)
    got = lax.all_to_all(sent, "col", 0, 0, tiled=True).reshape(CAP, TILE, width)
    source_tiles = got[place]
    target_tiles = target_group[cols_here]
    logits = (SHARPNESS / math.sqrt(width)) * jnp.einsum(
        "sid,sjd->sij", source_tiles, target_tiles, precision=HIGH
    )
    live = slots < cand_count[0, 0]
    row_onehot = rows_here[:, None] == jnp.arange(TD * col_count, dtype=jnp.int32)[None, :]
    col_onehot = cols_here[:, None] == jnp.arange(TD * row_count, dtype=jnp.int32)[None, :]
    row_grouped = row_onehot & live[:, None]
    col_grouped = col_onehot & live[:, None]
    col_pot = jnp.zeros((TD * row_count, TILE), F32)
    for _ in range(ITERS):
        col_slot = col_pot[cols_here]
        row_pot = everyone(tile_lse(slot_lse(logits + col_slot[:, None, :], 2), row_grouped), "col")
        row_slot = row_pot[rows_here]
        col_pot = everyone(tile_lse(slot_lse(logits + row_slot[:, :, None], 1), col_grouped), "row")
    row_slot = row_pot[rows_here]
    col_slot = col_pot[cols_here]
    log_plan = jnp.where(
        live[:, None, None], logits + row_slot[:, :, None] + col_slot[:, None, :], 0.0
    )
    return (
        log_plan[None, None],
        row_pot.reshape(1, col_count, -1),
        col_pot.reshape(row_count, 1, -1),
    )


def solution(mesh):
    both = ("row", "col")
    placed = (
        P(None, both, None),
        P(None, both, None, None, None),
        P(None, both, None),
        P(None, both),
        P(None, both, None),
        P(),
        P("row", "col", None, None),
        P("row", "col"),
    )
    return jax.shard_map(
        on_device,
        mesh=mesh,
        in_specs=placed,
        out_specs=(P("row", "col", None, None, None), P("row", None, None), P(None, "col", None)),
        check_vma=False,
    )
```

time: 703 us -> 431 us (0.61)
  matrix products: 154 us -> 7.76 us
  local copies, waits for them, and re-layouts: 171 us -> 42.3 us
  loops' own time: 75.8 us -> 0 us
  waiting for transfers between devices: 93.2 us -> 155 us
  other arithmetic: 77 us -> 21.6 us
  blocking collectives: 95.3 us -> 142 us
  Pallas kernels: 0 us -> 21.9 us
  starting transfers between devices: 15.6 us -> 24.2 us
    dot_general x56 -> x1, matrix products: 154 us -> 7.76 us  [on_device(): jnp.einsum('sid,sjd->sij', source_tiles, target_tiles, precision=HIGH)]
    all_to_all x2 -> x4, waiting for transfers between devices: 8.29 us -> 118 us  [the longest x1 85.8 us: on_device(): lax.all_to_all(sent, 'col', 0, 0, tiled=True).reshape(CAP, TILE, width)]
    gather x43 -> x8, local copies, waits for them, and re-layouts: 105 us -> 19.3 us  [the longest x1 6.45 us: on_device(): source_tiles = got[place]]
    another operation x2 -> x0, loops' own time: 75.8 us -> none  [aggregate(): lax.scan(add_block, (start_sum, start_deg), jnp.arange(block_vals.shape[1]))]
    all_gather x2 -> x1, waiting for transfers between devices: 84.8 us -> 37 us  [on_device(): lax.all_gather(target, 'row', axis=0, tiled=True).reshape(-1, TILE, width)]
    reduce_sum x44 -> x15, other arithmetic: 55.8 us -> 10.4 us  [the longest x4 5.74 us: slot_lse(): jnp.sum(jnp.exp(values - jnp.expand_dims(top, axis)), axis=axis)]
    all_gather x12 -> x5, blocking collectives: 76.9 us -> 122 us  [the longest x4 103 us: everyone(): return lax.all_gather(-merged(mine), axis, axis=0, tiled=True)]
    dynamic_slice x40 -> x0, local copies, waits for them, and re-layouts: 23.6 us -> none  [aggregate(): lax.scan(add_block, (start_sum, start_deg), jnp.arange(block_vals.shape[1]))]
  transfers between devices with their start and end apart: 4 -> 5, of which waited for: 2 -> 5; matrix products, arithmetic and copies ran while one was open for 27% -> 3% of each run, Pallas kernels for 0% -> 3%
where the time goes in v1:
time: 431 us; the launch traced here: 430 us
  waiting for transfers between devices  155 us (36%)
  blocking collectives  142 us (33%)
  local copies, waits for them, and re-layouts  42.3 us (10%)
  starting transfers between devices  24.2 us (6%)
  Pallas kernels  21.9 us (5%)
  other arithmetic  21.6 us (5%)
  between operations  15.2 us (4%)
  matrix products  7.76 us (2%)
    all_gather x4, blocking collectives, everyone(): return lax.all_gather(-merged(mine), axis, axis=0, tiled=True)  103 us
    all_to_all x1, waiting for transfers between devices, on_device(): lax.all_to_all(sent, 'col', 0, 0, tiled=True).reshape(CAP, TILE, width)  85.8 us
    all_gather x1, waiting for transfers between devices, on_device(): lax.all_gather(target, 'row', axis=0, tiled=True).reshape(-1, TILE, width)  37 us
    pallas_call x2, Pallas kernels, aggregate(): pl.pallas_call(aggregate_kernel, grid_spec=grid_spec, out_shape=jax.Shape...  21.9 us
    all_to_all x2, blocking collectives, everyone(): mine = lax.all_to_all(lse.reshape(size, TD, TILE), axis, 0, 0, tiled=True)  20.4 us
    all_gather x1, blocking collectives, on_device(): wanted = lax.all_gather(rows_here, 'col')  19.1 us
    all_to_all x1, waiting for transfers between devices, on_device(): ghost = lax.all_to_all(outgoing, ('row', 'col'), 0, 0, tiled=True)  19.1 us
    all_to_all x2, waiting for transfers between devices, everyone(): mine = lax.all_to_all(lse.reshape(size, TD, TILE), axis, 0, 0, tiled=True)  13.1 us
  transfers between devices with their start and end apart: 5, of which 5 were waited for; matrix products, arithmetic and copies ran while one was open for 3% of the time, Pallas kernels for 3%

profile of v1, /device:TPU:0, one launch (start us, length us, event | category | flops | bytes accessed | tf_op | source)
XLA Modules:
  0.0 430.2 jit_solution(8108387197681250910)
XLA Ops:
  8.5 6.3 %gather_fusion = f32[1024,256]{1,0:T(8,128)} fusion(f32[2048,256]{1,0:T(8,128)} %bitcast.68, s32[1024]{0:T(1024)S(1)} %broadcast_clamp_fusion), kind=kCustom, calls=%fused_computation | custom fusion | bytes 2101248 | tf_op jit(solution)/shard_map/gather | solution.py:151
  14.8 11.1 %all-to-all-start = ((f32[128,8,256]{2,1,0:T(8,128)}), f32[128,8,256]{2,1,0:T(8,128)S(1)}, u32[]{:S(2)}, u32[]{:S(2)}) async-start(f32[128,8,256]{2,1,0:T(8,128)} %bitcast.6), calls=%async_computation | async-start | bytes 2097152 | tf_op jit(solution)/shard_map/all_to_all | solution.py:152
  26.0 19.1 %all-to-all-done = f32[128,8,256]{2,1,0:T(8,128)S(1)} async-done(((f32[128,8,256]{2,1,0:T(8,128)}), f32[128,8,256]{2,1,0:T(8,128)S(1)}, u32[]{:S(2)}, u32[]{:S(2)}) %all-to-all-start) | async-done | bytes 1048608 | tf_op jit(solution)/shard_map/all_to_all | solution.py:152
  45.4 1.6 copy.22
  47.1 1.6 reshape.481.ghost_ref
  48.7 4.3 %copy-done.1 = bf16[2,8,20,128,128]{4,3,2,1,0:T(8,128)(2,1)S(1)} copy-done((bf16[2,8,20,128,128]{4,3,2,1,0:T(8,128)(2,1)S(1)}, bf16[2,8,20,128,128]{4,3,2,1,0:T(8,128)(2,1)}, u32[]{:S(2)}) %copy-start.1) | copy-done | bytes 10485784
  53.0 10.6 %aggregate.3 = f32[1024,256]{1,0:T(8,128)S(1)} custom-call(s32[8,20]{1,0:T(8,128)S(1)} %get-tuple-element.17.cols, s32[8]{0:T(128)S(1)} %get-tuple-element.25.count, bf16[2,8,20,128,128]{4,3,2,1,0:T(8,128)(2,1)S(1)} %copy-done.1, f32[2,1024,256]{2,1,0:T(8,128)S(1)} %copy-done, f32[2,512,256]{2,1,0:T(8,128)S(1)} %reshape.481.ghost_ref, f32[256,256]{1,0:T(8,128)S(1)} %copy-done.6), custom_call_target="tpu_custom_call" | custom-call | flops 2684354560 | bytes 8388608 | tf_op jit(solution)/shard_map/aggregate/pallas_call | solution.py:91
  64.7 19.1 %all-gather = s32[16,1,1,48]{3,2,1,0:T(1,128)S(1)} all-gather(s32[1,1,1,48]{3,2,1,0:T(1,128)S(1)} %get-tuple-element.21), channel_id=2, replica_groups=mesh['row'=8,'col'=16] {'col'}, dimensions={0}, use_global_device_ids=true | all-gather | bytes 3264 | tf_op jit(solution)/shard_map/all_gather | solution.py:136
  84.7 4.0 copy-done.2
  89.9 11.4 %aggregate.2 = f32[1024,256]{1,0:T(8,128)S(1)} custom-call(s32[8,20]{1,0:T(8,128)S(1)} %get-tuple-element.18.cols, s32[8]{0:T(128)S(1)} %get-tuple-element.26.count, bf16[2,8,20,128,128]{4,3,2,1,0:T(8,128)(2,1)S(1)} %copy-done.2, f32[2,1024,256]{2,1,0:T(8,128)S(1)} %copy-done, f32[2,512,256]{2,1,0:T(8,128)S(1)} %copy-done.4, f32[256,256]{1,0:T(8,128)S(1)} %copy-done.6), custom_call_target="tpu_custom_call" | custom-call | flops 2684354560 | bytes 8388608 | tf_op jit(solution)/shard_map/aggregate/pallas_call | solution.py:91
  101.3 3.7 gather_fusion.1
  105.0 5.2 %all-to-all-start.1 = ((f32[16,384,256]{2,1,0:T(8,128)}), f32[16,384,256]{2,1,0:T(8,128)}, u32[]{:S(2)}, u32[]{:S(2)}) async-start(f32[16,384,256]{2,1,0:T(8,128)} %bitcast.70), calls=%async_computation.1 | async-start | bytes 12582912 | tf_op jit(solution)/shard_map/all_to_all | solution.py:159
  111.9 85.8 %all-to-all-done.1 = f32[16,384,256]{2,1,0:T(8,128)} async-done(((f32[16,384,256]{2,1,0:T(8,128)}), f32[16,384,256]{2,1,0:T(8,128)}, u32[]{:S(2)}, u32[]{:S(2)}) %all-to-all-start.1) | async-done | bytes 6291488 | tf_op jit(solution)/shard_map/all_to_all | solution.py:159
  197.7 6.4 %gather_fusion.2 = f32[48,128,256]{2,1,0:T(8,128)} fusion(f32[48,128,256]{2,1,0:T(8,128)} %bitcast.13, s32[1024]{0:T(1024)S(1)} %get-tuple-element.30), kind=kCustom, calls=%fused_computation.2 | custom fusion | bytes 12583104 | tf_op jit(solution)/shard_map/gather | solution.py:160
  204.1 37.0 %all-gather.3.cloned.1.call-done = f32[8192,256]{1,0:T(8,128)} async-done(((f32[1024,256]{1,0:T(8,128)}), f32[8192,256]{1,0:T(8,128)}) %all-gather.3.cloned.1.call-update) | async-done | bytes 8388624 | tf_op jit(solution)/shard_map/all_gather | solution.py:156
  241.1 6.9 %gather_fusion.3 = f32[48,128,256]{2,1,0:T(8,128)} fusion(f32[64,128,256]{2,1,0:T(8,128)} %bitcast.71, s32[1024]{0:T(1024)S(1)} %get-tuple-element.29), kind=kCustom, calls=%fused_computation.3 | custom fusion | bytes 12583104 | tf_op jit(solution)/shard_map/gather | solution.py:161
  248.0 7.8 %add_reduce_fusion.2 = (f32[48,128]{1,0:T(8,128)S(1)}, f32[48,128,128]{2,1,0:T(8,128)S(1)}) fusion(f32[48,128]{1,0:T(8,128)S(1)} %gather_fusion.4, f32[48,128,256]{2,1,0:T(8,128)} %gather_fusion.2, f32[48,128,256]{2,1,0:T(8,128)} %gather_fusion.3), kind=kOutput, calls=%fused_computation.26 | convolution fusion | flops 1210312704 | bytes 15777792 | tf_op jit(solution)/shard_map/sid,sjd->sij/dot_general | solution.py:162
  255.7 1.9 exponential_reduce_fusion.3
  258.9 1.3 fusion.2
  260.8 4.5 %all-to-all-start.2 = ((f32[16,8,128]{2,1,0:T(8,128)}), f32[16,8,128]{2,1,0:T(8,128)S(1)}, u32[]{:S(2)}, u32[]{:S(2)}) async-start(f32[16,8,128]{2,1,0:T(8,128)} %select_bitcast_fusion.2), calls=%async_computation.2 | async-start | bytes 131072 | tf_op jit(solution)/shard_map/all_to_all | solution.py:122
  265.3 6.1 %all-to-all-done.2 = f32[16,8,128]{2,1,0:T(8,128)S(1)} async-done(((f32[16,8,128]{2,1,0:T(8,128)}), f32[16,8,128]{2,1,0:T(8,128)S(1)}, u32[]{:S(2)}, u32[]{:S(2)}) %all-to-all-start.2) | async-done | bytes 65568 | tf_op jit(solution)/shard_map/all_to_all | solution.py:122
  271.4 17.3 %all_gather.20 = f32[128,128]{1,0:T(8,128)S(1)} all-gather(f32[8,128]{1,0:T(8,128)S(1)} %add_negate_fusion.3), channel_id=1, replica_groups=mesh['row'=8,'col'=16] {'col'}, dimensions={0}, use_global_device_ids=true | all-gather | bytes 69632 | tf_op jit(solution)/shard_map/all_gather | solution.py:123
  292.6 11.7 %all_to_all.30 = f32[8,8,128]{2,1,0:T(8,128)S(1)} all-to-all(f32[8,8,128]{2,1,0:T(8,128)S(1)} %select_bitcast_fusion.4), channel_id=1, replica_groups=mesh['row'=8,'col'=16] {'row'}, dimensions={0} | all-to-all | bytes 65536 | tf_op jit(solution)/shard_map/all_to_all | solution.py:122
  304.3 34.1 %all_gather.21 = f32[64,128]{1,0:T(8,128)S(1)} all-gather(f32[8,128]{1,0:T(8,128)S(1)} %add_negate_fusion.2), channel_id=1, replica_groups=mesh['row'=8,'col'=16] {'row'}, dimensions={0}, use_global_device_ids=true | all-gather | bytes 36864 | tf_op jit(solution)/shard_map/all_gather | solution.py:123
  339.9 1.9 exponential_reduce_fusion.1
  343.0 1.3 fusion.5
  344.3 8.7 %all_to_all.31 = f32[16,8,128]{2,1,0:T(8,128)S(1)} all-to-all(f32[16,8,128]{2,1,0:T(8,128)S(1)} %select_bitcast_fusion.1), channel_id=1, replica_groups=mesh['row'=8,'col'=16] {'col'}, dimensions={0} | all-to-all | bytes 131072 | tf_op jit(solution)/shard_map/all_to_all | solution.py:122
  353.1 17.3 %all_gather.22 = f32[128,128]{1,0:T(8,128)S(1)} all-gather(f32[8,128]{1,0:T(8,128)S(1)} %add_negate_fusion.1), channel_id=1, replica_groups=mesh['row'=8,'col'=16] {'col'}, dimensions={0}, use_global_device_ids=true | all-gather | bytes 69632 | tf_op jit(solution)/shard_map/all_gather | solution.py:123
  374.8 3.3 all-to-all-start.5
  378.8 7.0 %all-to-all-done.5 = f32[8,8,128]{2,1,0:T(8,128)S(1)} async-done(((f32[8,8,128]{2,1,0:T(8,128)}), f32[8,8,128]{2,1,0:T(8,128)S(1)}, u32[]{:S(2)}, u32[]{:S(2)}) %all-to-all-start.5) | async-done | bytes 32800 | tf_op jit(solution)/shard_map/all_to_all | solution.py:122
  385.8 34.1 %all_gather.23 = f32[64,128]{1,0:T(8,128)S(1)} all-gather(f32[8,128]{1,0:T(8,128)S(1)} %add_negate_fusion), channel_id=1, replica_groups=mesh['row'=8,'col'=16] {'row'}, dimensions={0}, use_global_device_ids=true | all-gather | bytes 36864 | tf_op jit(solution)/shard_map/all_gather | solution.py:123
  420.5 2.2 select_bitcast_fusion
  (88 shorter events, 20.6 us)
Async XLA Ops:
  8.5 17.5 %copy-start.9 = (s32[2,8]{1,0:T(2,128)S(1)}, s32[2,8]{1,0:T(2,128)}, u32[]{:S(2)}) copy-start(s32[2,8]{1,0:T(2,128)} %param.11) | copy-start | bytes 196
  8.5 17.5 %copy-start.7 = (s32[2,8,20]{2,1,0:T(8,128)S(1)}, s32[2,8,20]{2,1,0:T(8,128)}, u32[]{:S(2)}) copy-start(s32[2,8,20]{2,1,0:T(8,128)} %param.10) | copy-start | bytes 3844
  14.8 30.3 %all-to-all-start = ((f32[128,8,256]{2,1,0:T(8,128)}), f32[128,8,256]{2,1,0:T(8,128)S(1)}, u32[]{:S(2)}, u32[]{:S(2)}) async-start(f32[128,8,256]{2,1,0:T(8,128)} %bitcast.6), calls=%async_computation | async-start | bytes 2097152 | tf_op jit(solution)/shard_map/all_to_all | solution.py:152
  25.9 215.2 %all-gather.3.cloned.1.call-start = ((), (), s32[]{:S(2)}) async-start(), calls=%async_computation.6 | async-start | bytes 9437184 | tf_op jit(solution)/shard_map/all_gather | solution.py:156
  26.0 22.7 %copy-start = (f32[2,1024,256]{2,1,0:T(8,128)S(1)}, f32[2,1024,256]{2,1,0:T(8,128)}, u32[]{:S(2)}) copy-start(f32[2,1024,256]{2,1,0:T(8,128)} %own_ref.3) | copy-start | bytes 6291460
  26.0 22.7 %copy-start.6 = (f32[256,256]{1,0:T(8,128)S(1)}, f32[256,256]{1,0:T(8,128)}, u32[]{:S(2)}) copy-start(f32[256,256]{1,0:T(8,128)} %weight_ref.3) | copy-start | bytes 786436
  48.7 15.0 %copy-start.3 = (f32[2,512,256]{2,1,0:T(8,128)}, f32[2,512,256]{2,1,0:T(8,128)S(1)}, u32[]{:S(2)}) copy-start(f32[2,512,256]{2,1,0:T(8,128)S(1)} %reshape.481.ghost_ref) | copy-start | bytes 3145732
  48.7 4.3 %copy-start.1 = (bf16[2,8,20,128,128]{4,3,2,1,0:T(8,128)(2,1)S(1)}, bf16[2,8,20,128,128]{4,3,2,1,0:T(8,128)(2,1)}, u32[]{:S(2)}) copy-start(bf16[2,8,20,128,128]{4,3,2,1,0:T(8,128)(2,1)} %adj_ref.3) | copy-start | bytes 31457284
  53.0 11.6 %copy-start.8 = (s32[1,1,2,48]{3,2,1,0:T(2,128)S(1)}, s32[1,1,2,48]{3,2,1,0:T(2,128)}, u32[]{:S(2)}) copy-start(s32[1,1,2,48]{3,2,1,0:T(2,128)} %param.14) | copy-start | bytes 1156
  63.6 1.0 copy-start.5
  84.7 4.0 copy-start.2
  88.7 1.2 copy-start.4
  105.0 92.7 %all-to-all-start.1 = ((f32[16,384,256]{2,1,0:T(8,128)}), f32[16,384,256]{2,1,0:T(8,128)}, u32[]{:S(2)}, u32[]{:S(2)}) async-start(f32[16,384,256]{2,1,0:T(8,128)} %bitcast.70), calls=%async_computation.1 | async-start | bytes 12582912 | tf_op jit(solution)/shard_map/all_to_all | solution.py:159
  260.8 10.6 %all-to-all-start.2 = ((f32[16,8,128]{2,1,0:T(8,128)}), f32[16,8,128]{2,1,0:T(8,128)S(1)}, u32[]{:S(2)}, u32[]{:S(2)}) async-start(f32[16,8,128]{2,1,0:T(8,128)} %select_bitcast_fusion.2), calls=%async_computation.2 | async-start | bytes 131072 | tf_op jit(solution)/shard_map/all_to_all | solution.py:122
  374.8 11.0 %all-to-all-start.5 = ((f32[8,8,128]{2,1,0:T(8,128)}), f32[8,8,128]{2,1,0:T(8,128)S(1)}, u32[]{:S(2)}, u32[]{:S(2)}) async-start(f32[8,8,128]{2,1,0:T(8,128)} %select_bitcast_fusion.3), calls=%async_computation.5 | async-start | bytes 65536 | tf_op jit(solution)/shard_map/all_to_all | solution.py:122
Sparse Core Ops, SparseCore 0:
  64.8 176.2 all-gather.2

commit v2 on v1

--- a/solution.py
+++ b/solution.py
@@ -11,7 +11,6 @@
 TD = 8
 CAP = 48
 ITERS = 2
-HIGH = lax.Precision.HIGH
 SHARPNESS = 2.0
 NEGATIVE = -1e30
 F32 = jnp.float32
@@ -105,22 +104,206 @@
     return top + jnp.log(jnp.sum(jnp.exp(parts - top[None]), axis=0))
 
 
-def tile_lse(slot_lse, grouped):
-    spread = jnp.where(grouped[:, :, None], slot_lse[:, None, :], NEGATIVE)
-    top = jnp.max(spread, axis=0)
-    total = jnp.sum(jnp.where(grouped[:, :, None], jnp.exp(spread - top[None]), 0.0), axis=0)
-    return jnp.where(total > 0.0, top + jnp.log(jnp.maximum(total, 1e-30)), NEGATIVE)
-
-
-def slot_lse(values, axis):
-    top = jnp.max(values, axis=axis)
-    return top + jnp.log(jnp.sum(jnp.exp(values - jnp.expand_dims(top, axis)), axis=axis))
-
-
-def everyone(lse, axis):
+def exchange(stage, axis, source, landing, sends, arrivals):
     size = lax.axis_size(axis)
-    mine = lax.all_to_all(lse.reshape(size, TD, TILE), axis, 0, 0, tiled=True)
-    return lax.all_gather(-merged(mine), axis, axis=0, tiled=True)
+    me = lax.axis_index(axis)
+
+    def copy_to(d, landed):
+        peer = lax.rem(me + d, size)
+        return pltpu.make_async_remote_copy(
+            src_ref=source(peer),
+            dst_ref=landing(landed),
+            send_sem=sends.at[stage, d],
+            recv_sem=arrivals.at[stage, d],
+            device_id={axis: peer},
+            device_id_type=pl.DeviceIdType.MESH,
+        )
+
+    def start(d, carry):
+        copy_to(d, me).start()
+        return carry
+
+    def finish(d, carry):
+        copy_to(d, me).wait_send()
+        copy_to(d, lax.rem(me - d + size, size)).wait_recv()
+        return carry
+
+    lax.fori_loop(1, size, start, 0)
+    lax.fori_loop(1, size, finish, 0)
+
+
+def sinkhorn_kernel(
+    info, got, group, plan, row_out, col_out, lse, tiles, row_in, row_all, col_in, col_all, sends, arrivals
+):
+    row_count = lax.axis_size("row")
+    col_count = lax.axis_size("col")
+    my_row = lax.axis_index("row")
+    my_col = lax.axis_index("col")
+    width = got.shape[2]
+    barrier = pltpu.get_barrier_semaphore()
+
+    def greet(axis):
+        size = lax.axis_size(axis)
+
+        def signal(d, carry):
+            peer = lax.rem(lax.axis_index(axis) + d, size)
+            pl.semaphore_signal(
+                barrier, inc=1, device_id={axis: peer}, device_id_type=pl.DeviceIdType.MESH
+            )
+            return carry
+
+        lax.fori_loop(1, size, signal, 0)
+
+    greet("row")
+    greet("col")
+
+    def logit(i, carry):
+        for k in range(4):
+            s = 4 * i + k
+            ah, al = split_two(got[info[2, s]])
+            bh, bl = split_two(group[info[1, s]])
+            left = jnp.concatenate([ah, ah, al], axis=1)
+            right = jnp.concatenate([bh, bl, bh], axis=1)
+            both = lax.dot_general(left, right, (((1,), (1,)), ((), ())), preferred_element_type=F32)
+            plan[s] = both * (SHARPNESS / math.sqrt(width))
+        return carry
+
+    lax.fori_loop(0, CAP // 4, logit, 0)
+    pl.semaphore_wait(barrier, row_count + col_count - 2)
+
+    lanes = lax.broadcasted_iota(jnp.int32, (TILE, TILE), 1)
+
+    def along_lanes(it):
+        def eight(g, carry):
+            tops = jnp.zeros((TILE, TILE), F32)
+            sums = jnp.ones((TILE, TILE), F32)
+            for k in range(8):
+                s = 8 * g + k
+                x = plan[s]
+                if it > 0:
+                    x = x + col_all[it - 1, pl.ds(info[1, s], 1), :]
+                top = jnp.max(x, axis=1, keepdims=True)
+                total = jnp.sum(jnp.exp(x - top), axis=1, keepdims=True)
+                tops = jnp.where(lanes == k, top, tops)
+                sums = jnp.where(lanes == k, total, sums)
+            lse[pl.ds(8 * g, 8), :] = (jnp.transpose(tops) + jnp.log(jnp.transpose(sums)))[:8]
+            return carry
+
+        lax.fori_loop(0, CAP // 8, eight, 0)
+
+    def columns(it, g):
+        rows = [row_all[it, pl.ds(info[0, 8 * g + k], 1), :] for k in range(8)]
+        rows = jnp.concatenate(rows, axis=0)
+        return jnp.transpose(jnp.concatenate([rows] * (TILE // 8), axis=0))
+
+    def along_rows(it):
+        def eight(g, carry):
+            pots = columns(it, g)
+            tops, sums = [], []
+            for k in range(8):
+                x = plan[8 * g + k] + pots[:, k : k + 1]
+                top = jnp.max(x, axis=0, keepdims=True)
+                tops.append(top)
+                sums.append(jnp.sum(jnp.exp(x - top), axis=0, keepdims=True))
+            lse[pl.ds(8 * g, 8), :] = jnp.concatenate(tops, axis=0) + jnp.log(jnp.concatenate(sums, axis=0))
+            return carry
+
+        lax.fori_loop(0, CAP // 8, eight, 0)
+
+    def by_tile(which, count):
+        number = lax.broadcasted_iota(jnp.int32, (count, TILE), 0)
+
+        def largest(i, top):
+            for k in range(4):
+                s = 4 * i + k
+                top = jnp.maximum(top, jnp.where(number == info[which + 3, s], lse[pl.ds(s, 1), :], NEGATIVE))
+            return top
+
+        top = lax.fori_loop(0, CAP // 4, largest, jnp.full((count, TILE), NEGATIVE, F32))
+        tiles[:count] = top
+
+        def add(i, total):
+            for k in range(4):
+                s = 4 * i + k
+                term = jnp.exp(lse[pl.ds(s, 1), :] - tiles[pl.ds(info[which, s], 1), :])
+                total = total + jnp.where(number == info[which + 3, s], term, 0.0)
+            return total
+
+        total = lax.fori_loop(0, CAP // 4, add, jnp.zeros((count, TILE), F32))
+        tiles[:count] = jnp.where(total > 0.0, top + jnp.log(jnp.maximum(total, 1e-30)), NEGATIVE)
+
+    def settle(it, stage, axis, inward, everyone):
+        me = lax.axis_index(axis)
+        mine = pl.ds(pl.multiple_of(me * TD, TD), TD)
+        inward[it, me] = tiles[mine, :]
+        exchange(
+            stage,
+            axis,
+            lambda peer: tiles.at[pl.ds(pl.multiple_of(peer * TD, TD), TD), :],
+            lambda owner: inward.at[it, owner],
+            sends,
+            arrivals,
+        )
+        everyone[it, mine, :] = -merged(inward[it])
+        exchange(
+            stage + 1,
+            axis,
+            lambda peer: everyone.at[it, mine, :],
+            lambda owner: everyone.at[it, pl.ds(pl.multiple_of(owner * TD, TD), TD), :],
+            sends,
+            arrivals,
+        )
+
+    for it in range(ITERS):
+        along_lanes(it)
+        by_tile(0, TD * col_count)
+        settle(it, 4 * it, "col", row_in, row_all)
+        along_rows(it)
+        by_tile(1, TD * row_count)
+        settle(it, 4 * it + 2, "row", col_in, col_all)
+
+    row_out[...] = row_all[ITERS - 1]
+    col_out[...] = col_all[ITERS - 1]
+
+    def finish(g, carry):
+        pots = columns(ITERS - 1, g)
+        for k in range(8):
+            s = 8 * g + k
+            x = plan[s] + pots[:, k : k + 1] + col_all[ITERS - 1, pl.ds(info[1, s], 1), :]
+            plan[s] = jnp.where(jnp.full((TILE, TILE), info[5, s], jnp.int32) > 0, x, 0.0)
+        return carry
+
+    lax.fori_loop(0, CAP // 8, finish, 0)
+
+
+def sinkhorn(info, got, group):
+    row_count = lax.axis_size("row")
+    col_count = lax.axis_size("col")
+    vmem = pl.BlockSpec(memory_space=pltpu.VMEM)
+    return pl.pallas_call(
+        sinkhorn_kernel,
+        in_specs=[pl.BlockSpec(memory_space=pltpu.SMEM), vmem, vmem],
+        out_specs=[vmem] * 3,
+        out_shape=[
+            jax.ShapeDtypeStruct((CAP, TILE, TILE), F32),
+            jax.ShapeDtypeStruct((TD * col_count, TILE), F32),
+            jax.ShapeDtypeStruct((TD * row_count, TILE), F32),
+        ],
+        scratch_shapes=[
+            pltpu.VMEM((CAP, TILE), F32),
+            pltpu.VMEM((TD * max(row_count, col_count), TILE), F32),
+            pltpu.VMEM((ITERS, col_count, TD, TILE), F32),
+            pltpu.VMEM((ITERS, TD * col_count, TILE), F32),
+            pltpu.VMEM((ITERS, row_count, TD, TILE), F32),
+            pltpu.VMEM((ITERS, TD * row_count, TILE), F32),
+            pltpu.SemaphoreType.DMA((4 * ITERS, max(row_count, col_count))),
+            pltpu.SemaphoreType.DMA((4 * ITERS, max(row_count, col_count))),
+        ],
+        compiler_params=pltpu.CompilerParams(
+            collective_id=0, has_side_effects=True, vmem_limit_bytes=40 * 2**20
+        ),
+        name="sinkhorn",
+    )(info, got, group)
 
 
 def on_device(features, adj_vals, blk_cols, blk_count, send_list, weight, cand_tiles, cand_count):
@@ -157,27 +340,18 @@
     source = aggregate(features, ghost, adj_vals, blk_cols, blk_count, weight, 0)
     sent = source.reshape(TD, TILE, width)[asked.reshape(-1)].reshape(col_count, share * TILE, width)
     got = lax.all_to_all(sent, "col", 0, 0, tiled=True).reshape(CAP, TILE, width)
-    source_tiles = got[place]
-    target_tiles = target_group[cols_here]
-    logits = (SHARPNESS / math.sqrt(width)) * jnp.einsum(
-        "sid,sjd->sij", source_tiles, target_tiles, precision=HIGH
-    )
     live = slots < cand_count[0, 0]
-    row_onehot = rows_here[:, None] == jnp.arange(TD * col_count, dtype=jnp.int32)[None, :]
-    col_onehot = cols_here[:, None] == jnp.arange(TD * row_count, dtype=jnp.int32)[None, :]
-    row_grouped = row_onehot & live[:, None]
-    col_grouped = col_onehot & live[:, None]
-    col_pot = jnp.zeros((TD * row_count, TILE), F32)
-    for _ in range(ITERS):
-        col_slot = col_pot[cols_here]
-        row_pot = everyone(tile_lse(slot_lse(logits + col_slot[:, None, :], 2), row_grouped), "col")
-        row_slot = row_pot[rows_here]
-        col_pot = everyone(tile_lse(slot_lse(logits + row_slot[:, :, None], 1), col_grouped), "row")
-    row_slot = row_pot[rows_here]
-    col_slot = col_pot[cols_here]
-    log_plan = jnp.where(
-        live[:, None, None], logits + row_slot[:, :, None] + col_slot[:, None, :], 0.0
-    )
+    info = jnp.stack(
+        [
+            rows_here,
+            cols_here,
+            place,
+            jnp.where(live, rows_here, -1),
+            jnp.where(live, cols_here, -1),
+            live.astype(jnp.int32),
+        ]
+    )
+    log_plan, row_pot, col_pot = sinkhorn(info, got, target_group)
     return (
         log_plan[None, None],
         row_pot.reshape(1, col_count, -1),

time: 431 us -> 317 us (0.74)
  blocking collectives: 142 us -> 17 us
  Pallas kernels: 21.9 us -> 94.5 us
  other arithmetic: 21.6 us -> 1.69 us
  local copies, waits for them, and re-layouts: 42.3 us -> 27.5 us
  waiting for transfers between devices: 155 us -> 145 us
  starting transfers between devices: 24.2 us -> 15.8 us
  matrix products: 7.76 us -> 0 us
    all_gather x4 -> x0, blocking collectives: 103 us -> none  [everyone(): return lax.all_gather(-merged(mine), axis, axis=0, tiled=True)]
    pallas_call x0 -> x1, Pallas kernels: none -> 66.4 us  [sinkhorn(): pl.pallas_call(sinkhorn_kernel, in_specs=[pl.BlockSpec(memory_space=pltpu...]
    all_to_all x2 -> x0, blocking collectives: 20.4 us -> none  [everyone(): mine = lax.all_to_all(lse.reshape(size, TD, TILE), axis, 0, 0, tiled=True)]
    gather x7 -> x0, local copies, waits for them, and re-layouts: 16.3 us -> none  [the longest x1 6.89 us: on_device(): target_tiles = target_group[cols_here]]
    all_to_all x2 -> x0, waiting for transfers between devices: 13.1 us -> none  [everyone(): mine = lax.all_to_all(lse.reshape(size, TD, TILE), axis, 0, 0, tiled=True)]
    reduce_sum x12 -> x0, other arithmetic: 9.59 us -> none  [the longest x4 5.74 us: slot_lse(): jnp.sum(jnp.exp(values - jnp.expand_dims(top, axis)), axis=axis)]
    all_to_all x2 -> x0, starting transfers between devices: 7.8 us -> none  [everyone(): mine = lax.all_to_all(lse.reshape(size, TD, TILE), axis, 0, 0, tiled=True)]
    dot_general x1 -> x0, matrix products: 7.76 us -> none  [on_device(): jnp.einsum('sid,sjd->sij', source_tiles, target_tiles, precision=HIGH)]
  transfers between devices with their start and end apart: 5 -> 3, of which waited for: 5 -> 3; matrix products, arithmetic and copies ran while one was open for 3% -> 1% of each run, Pallas kernels for 3% -> 5%
where the time goes in v2:
time: 317 us; the launch traced here: 316 us
  waiting for transfers between devices  145 us (46%)
  Pallas kernels  94.5 us (30%)
  local copies, waits for them, and re-layouts  27.5 us (9%)
  blocking collectives  17 us (5%)
  starting transfers between devices  15.8 us (5%)
  between operations  14.9 us (5%)
    all_to_all x1, waiting for transfers between devices, on_device(): lax.all_to_all(sent, 'col', 0, 0, tiled=True).reshape(CAP, TILE, width)  86.3 us
    pallas_call x1, Pallas kernels, sinkhorn(): pl.pallas_call(sinkhorn_kernel, in_specs=[pl.BlockSpec(memory_space=pltpu...  66.4 us
    all_gather x1, waiting for transfers between devices, on_device(): lax.all_gather(target, 'row', axis=0, tiled=True).reshape(-1, TILE, width)  39.5 us
    pallas_call x2, Pallas kernels, aggregate(): pl.pallas_call(aggregate_kernel, grid_spec=grid_spec, out_shape=jax.Shape...  28.1 us
    all_to_all x1, waiting for transfers between devices, on_device(): ghost = lax.all_to_all(outgoing, ('row', 'col'), 0, 0, tiled=True)  19.1 us
    all_gather x1, blocking collectives, on_device(): wanted = lax.all_gather(rows_here, 'col')  17 us
    unnamed x22, local copies, waits for them, and re-layouts  12.9 us
    all_to_all x1, starting transfers between devices, on_device(): ghost = lax.all_to_all(outgoing, ('row', 'col'), 0, 0, tiled=True)  11.1 us
  transfers between devices with their start and end apart: 3, of which 3 were waited for; matrix products, arithmetic and copies ran while one was open for 1% of the time, Pallas kernels for 5%

profile of v2, /device:TPU:0, one launch (start us, length us, event | category | flops | bytes accessed | tf_op | source)
XLA Modules:
  0.0 316.3 jit_solution(9989935915687588710)
XLA Ops:
  7.2 0.7 reduce
  7.9 0.1 squeeze.26
  8.1 0.1 add_bitcast_fusion
  8.1 0.1 copy.20
  8.2 0.2 reshape.280
  8.5 6.3 %gather_fusion = f32[1024,256]{1,0:T(8,128)} fusion(f32[2048,256]{1,0:T(8,128)} %bitcast.48, s32[1024]{0:T(1024)S(1)} %broadcast_clamp_fusion), kind=kCustom, calls=%fused_computation | custom fusion | bytes 2101248 | tf_op jit(solution)/shard_map/gather | solution.py:334
  14.7 11.1 %all-to-all-start = ((f32[128,8,256]{2,1,0:T(8,128)}), f32[128,8,256]{2,1,0:T(8,128)S(1)}, u32[]{:S(2)}, u32[]{:S(2)}) async-start(f32[128,8,256]{2,1,0:T(8,128)} %bitcast.10), calls=%async_computation | async-start | bytes 2097152 | tf_op jit(solution)/shard_map/all_to_all | solution.py:335
  25.9 0.0 all-gather.3.cloned.1.call-start
  26.0 19.1 %all-to-all-done = f32[128,8,256]{2,1,0:T(8,128)S(1)} async-done(((f32[128,8,256]{2,1,0:T(8,128)}), f32[128,8,256]{2,1,0:T(8,128)S(1)}, u32[]{:S(2)}, u32[]{:S(2)}) %all-to-all-start) | async-done | bytes 1048608 | tf_op jit(solution)/shard_map/all_to_all | solution.py:335
  45.1 0.3 copy.21
  45.4 1.6 copy.22
  47.1 1.6 reshape.283.ghost_ref
  48.7 4.3 %copy-done.1 = bf16[2,8,20,128,128]{4,3,2,1,0:T(8,128)(2,1)S(1)} copy-done((bf16[2,8,20,128,128]{4,3,2,1,0:T(8,128)(2,1)S(1)}, bf16[2,8,20,128,128]{4,3,2,1,0:T(8,128)(2,1)}, u32[]{:S(2)}) %copy-start.1) | copy-done | bytes 10485784
  53.0 13.1 %aggregate.3 = f32[1024,256]{1,0:T(8,128)S(1)} custom-call(s32[8,20]{1,0:T(8,128)S(1)} %get-tuple-element.23.cols, s32[8]{0:T(128)S(1)} %get-tuple-element.25.count, bf16[2,8,20,128,128]{4,3,2,1,0:T(8,128)(2,1)S(1)} %copy-done.1, f32[2,1024,256]{2,1,0:T(8,128)S(1)} %copy-done, f32[2,512,256]{2,1,0:T(8,128)S(1)} %reshape.283.ghost_ref, f32[256,256]{1,0:T(8,128)S(1)} %copy-done.6), custom_call_target="tpu_custom_call" | custom-call | flops 2684354560 | bytes 8388608 | tf_op jit(solution)/shard_map/aggregate/pallas_call | solution.py:90
  66.2 1.0 copy-done.5
  67.2 17.0 %all-gather = s32[16,1,1,48]{3,2,1,0:T(1,128)S(1)} all-gather(s32[1,1,1,48]{3,2,1,0:T(1,128)S(1)} %get-tuple-element.27), channel_id=2, replica_groups=mesh['row'=8,'col'=16] {'col'}, dimensions={0}, use_global_device_ids=true | all-gather | bytes 3264 | tf_op jit(solution)/shard_map/all_gather | solution.py:319
  84.2 0.5 convert_reduce_fusion
  84.7 0.1 select_reduce_fusion
  84.8 0.1 copy.23
  84.9 0.1 reshape.285
  85.1 4.0 %copy-done.2 = bf16[2,8,20,128,128]{4,3,2,1,0:T(8,128)(2,1)S(1)} copy-done((bf16[2,8,20,128,128]{4,3,2,1,0:T(8,128)(2,1)S(1)}, bf16[2,8,20,128,128]{4,3,2,1,0:T(8,128)(2,1)}, u32[]{:S(2)}) %copy-start.2) | copy-done | bytes 10485784
  89.1 1.2 copy-done.4
  90.3 15.0 %aggregate.2 = f32[1024,256]{1,0:T(8,128)S(1)} custom-call(s32[8,20]{1,0:T(8,128)S(1)} %get-tuple-element.24.cols, s32[8]{0:T(128)S(1)} %get-tuple-element.26.count, bf16[2,8,20,128,128]{4,3,2,1,0:T(8,128)(2,1)S(1)} %copy-done.2, f32[2,1024,256]{2,1,0:T(8,128)S(1)} %copy-done, f32[2,512,256]{2,1,0:T(8,128)S(1)} %copy-done.4, f32[256,256]{1,0:T(8,128)S(1)} %copy-done.6), custom_call_target="tpu_custom_call" | custom-call | flops 2684354560 | bytes 8388608 | tf_op jit(solution)/shard_map/aggregate/pallas_call | solution.py:90
  105.3 3.5 %gather_fusion.1 = f32[48,128,256]{2,1,0:T(8,128)} fusion(f32[8,128,256]{2,1,0:T(8,128)S(1)} %bitcast.49, s32[1024]{0:T(1024)S(1)} %pad_clamp_fusion), kind=kCustom, calls=%fused_computation.1 | custom fusion | bytes 12583104 | tf_op jit(solution)/shard_map/gather | solution.py:341
  108.9 4.6 %all-to-all-start.1 = ((f32[16,384,256]{2,1,0:T(8,128)}), f32[16,384,256]{2,1,0:T(8,128)}, u32[]{:S(2)}, u32[]{:S(2)}) async-start(f32[16,384,256]{2,1,0:T(8,128)} %bitcast.52), calls=%async_computation.1 | async-start | bytes 12582912 | tf_op jit(solution)/shard_map/all_to_all | solution.py:342
  114.2 0.2 convert_reduce_fusion.1
  114.4 86.3 %all-to-all-done.1 = f32[16,384,256]{2,1,0:T(8,128)} async-done(((f32[16,384,256]{2,1,0:T(8,128)}), f32[16,384,256]{2,1,0:T(8,128)}, u32[]{:S(2)}, u32[]{:S(2)}) %all-to-all-start.1) | async-done | bytes 6291488 | tf_op jit(solution)/shard_map/all_to_all | solution.py:342
  200.7 39.5 %all-gather.3.cloned.1.call-done = f32[8192,256]{1,0:T(8,128)} async-done(((f32[1024,256]{1,0:T(8,128)}), f32[8192,256]{1,0:T(8,128)}) %all-gather.3.cloned.1.call-update) | async-done | bytes 8388624 | tf_op jit(solution)/shard_map/all_gather | solution.py:339
  240.1 66.4 %sinkhorn.1 = (f32[48,128,128]{2,1,0:T(8,128)S(1)}, f32[128,128]{1,0:T(8,128)S(1)}, f32[64,128]{1,0:T(8,128)S(1)}) custom-call(s32[6,48]{1,0:T(8,128)S(1)} %stack.2.info, f32[48,128,256]{2,1,0:T(8,128)} %bitcast.17.got, f32[64,128,256]{2,1,0:T(8,128)} %bitcast.53), custom_call_target="tpu_custom_call" | custom-call | tf_op jit(solution)/shard_map/sinkhorn/pallas_call | solution.py:283
  306.5 0.6 reshape.289
  307.2 1.7 copy.28
  308.9 0.6 copy.29
  (32 shorter events, 0.2 us)
Async XLA Ops:
  7.2 18.8 %copy-start.9 = (s32[2,8]{1,0:T(2,128)S(1)}, s32[2,8]{1,0:T(2,128)}, u32[]{:S(2)}) copy-start(s32[2,8]{1,0:T(2,128)} %param.11) | copy-start | bytes 196
  7.2 18.8 %copy-start.7 = (s32[2,8,20]{2,1,0:T(8,128)S(1)}, s32[2,8,20]{2,1,0:T(8,128)}, u32[]{:S(2)}) copy-start(s32[2,8,20]{2,1,0:T(8,128)} %param.10) | copy-start | bytes 3844
  14.7 33.9 %copy-start = (f32[2,1024,256]{2,1,0:T(8,128)S(1)}, f32[2,1024,256]{2,1,0:T(8,128)}, u32[]{:S(2)}) copy-start(f32[2,1024,256]{2,1,0:T(8,128)} %own_ref.3) | copy-start | bytes 6291460
  14.7 33.9 %copy-start.6 = (f32[256,256]{1,0:T(8,128)S(1)}, f32[256,256]{1,0:T(8,128)}, u32[]{:S(2)}) copy-start(f32[256,256]{1,0:T(8,128)} %weight_ref.3) | copy-start | bytes 786436
  14.7 30.3 %all-to-all-start = ((f32[128,8,256]{2,1,0:T(8,128)}), f32[128,8,256]{2,1,0:T(8,128)S(1)}, u32[]{:S(2)}, u32[]{:S(2)}) async-start(f32[128,8,256]{2,1,0:T(8,128)} %bitcast.10), calls=%async_computation | async-start | bytes 2097152 | tf_op jit(solution)/shard_map/all_to_all | solution.py:335
  25.9 214.2 %all-gather.3.cloned.1.call-start = ((), (), s32[]{:S(2)}) async-start(), calls=%async_computation.2 | async-start | bytes 9437184 | tf_op jit(solution)/shard_map/all_gather | solution.py:339
  48.7 17.5 %copy-start.3 = (f32[2,512,256]{2,1,0:T(8,128)}, f32[2,512,256]{2,1,0:T(8,128)S(1)}, u32[]{:S(2)}) copy-start(f32[2,512,256]{2,1,0:T(8,128)S(1)} %reshape.283.ghost_ref) | copy-start | bytes 3145732
  48.7 4.3 %copy-start.1 = (bf16[2,8,20,128,128]{4,3,2,1,0:T(8,128)(2,1)S(1)}, bf16[2,8,20,128,128]{4,3,2,1,0:T(8,128)(2,1)}, u32[]{:S(2)}) copy-start(bf16[2,8,20,128,128]{4,3,2,1,0:T(8,128)(2,1)} %adj_ref.3) | copy-start | bytes 31457284
  53.0 14.1 %copy-start.8 = (s32[1,1,2,48]{3,2,1,0:T(2,128)S(1)}, s32[1,1,2,48]{3,2,1,0:T(2,128)}, u32[]{:S(2)}) copy-start(s32[1,1,2,48]{3,2,1,0:T(2,128)} %param.14) | copy-start | bytes 1156
  66.2 1.0 copy-start.5
  85.0 4.0 %copy-start.2 = (bf16[2,8,20,128,128]{4,3,2,1,0:T(8,128)(2,1)S(1)}, bf16[2,8,20,128,128]{4,3,2,1,0:T(8,128)(2,1)}, u32[]{:S(2)}) copy-start(bf16[2,8,20,128,128]{4,3,2,1,0:T(8,128)(2,1)} %adj_ref.3) | copy-start | bytes 31457284
  89.1 1.2 copy-start.4
  108.9 91.8 %all-to-all-start.1 = ((f32[16,384,256]{2,1,0:T(8,128)}), f32[16,384,256]{2,1,0:T(8,128)}, u32[]{:S(2)}, u32[]{:S(2)}) async-start(f32[16,384,256]{2,1,0:T(8,128)} %bitcast.52), calls=%async_computation.1 | async-start | bytes 12582912 | tf_op jit(solution)/shard_map/all_to_all | solution.py:342
Sparse Core Ops, SparseCore 0:
  67.3 172.8 all-gather.2

commit v3 on v2

--- a/solution.py
+++ b/solution.py
@@ -23,7 +23,8 @@
 
 
 def aggregate_kernel(cols, count, adj_ref, own_ref, ghost_ref, weight_ref, out_ref, table, wstack, acc, deg):
-    t = pl.program_id(0)
+    g = pl.program_id(0)
+    t = pl.program_id(1)
     own_rows, width = own_ref.shape
 
     @pl.when(t == 0)
@@ -43,15 +44,15 @@
 
     acc[...] = jnp.zeros_like(acc)
     deg[...] = jnp.zeros_like(deg)
-    n = count[t]
+    n = count[g, t]
 
     def pair(i, carry):
         b = 2 * i
         first = adj_ref[0, b]
         second = adj_ref[0, b + 1]
         second = jnp.where(b + 1 < n, second, jnp.zeros_like(second))
-        one = table[pl.ds(pl.multiple_of(cols[t, b] * TILE, TILE), TILE), :]
-        two = table[pl.ds(pl.multiple_of(cols[t, b + 1] * TILE, TILE), TILE), :]
+        one = table[pl.ds(pl.multiple_of(cols[g, t, b] * TILE, TILE), TILE), :]
+        two = table[pl.ds(pl.multiple_of(cols[g, t, b + 1] * TILE, TILE), TILE), :]
         left = jnp.concatenate([first, second], axis=1)
         right = jnp.concatenate([one, two], axis=0)
         acc[...] += jnp.dot(left, right, preferred_element_type=F32)
@@ -67,19 +68,19 @@
     out_ref[...] = own + jnp.maximum(mixed, 0.0)
 
 
-def aggregate(own, ghost, adj, cols, count, weight, graph):
-    rows, width = own.shape[1:]
+def aggregate(own, ghost, adj, cols, count, weight):
+    graphs, rows, width = own.shape
     tiles, blocks = adj.shape[1:3]
     grid_spec = pltpu.PrefetchScalarGridSpec(
         num_scalar_prefetch=2,
-        grid=(tiles,),
+        grid=(graphs, tiles),
         in_specs=[
-            pl.BlockSpec((None, 1, blocks, TILE, TILE), lambda t, *_: (graph, t, 0, 0, 0)),
-            pl.BlockSpec((None, rows, width), lambda t, *_: (graph, 0, 0)),
-            pl.BlockSpec((None, ghost.shape[1], width), lambda t, *_: (graph, 0, 0)),
-            pl.BlockSpec((width, width), lambda t, *_: (0, 0)),
+            pl.BlockSpec((None, 1, blocks, TILE, TILE), lambda g, t, *_: (g, t, 0, 0, 0)),
+            pl.BlockSpec((None, rows, width), lambda g, t, *_: (g, 0, 0)),
+            pl.BlockSpec((None, ghost.shape[1], width), lambda g, t, *_: (g, 0, 0)),
+            pl.BlockSpec((width, width), lambda g, t, *_: (0, 0)),
         ],
-        out_specs=pl.BlockSpec((TILE, width), lambda t, *_: (t, 0)),
+        out_specs=pl.BlockSpec((None, TILE, width), lambda g, t, *_: (g, t, 0)),
         scratch_shapes=[
             pltpu.VMEM((rows + ghost.shape[1], 2 * width), BF16),
             pltpu.VMEM((3 * width, width), BF16),
@@ -90,13 +91,15 @@
     return pl.pallas_call(
         aggregate_kernel,
         grid_spec=grid_spec,
-        out_shape=jax.ShapeDtypeStruct((rows, width), F32),
+        out_shape=jax.ShapeDtypeStruct((graphs, rows, width), F32),
         compiler_params=pltpu.CompilerParams(vmem_limit_bytes=24 * 2**20),
         cost_estimate=pl.CostEstimate(
-            flops=tiles * blocks * TILE * TILE * width * 4, bytes_accessed=8 * 2**20, transcendentals=0
+            flops=graphs * tiles * blocks * TILE * TILE * width * 4,
+            bytes_accessed=16 * 2**20,
+            transcendentals=0,
         ),
         name="aggregate",
-    )(cols[graph], count[graph], adj, own, ghost, weight)
+    )(cols, count, adj, own, ghost, weight)
 
 
 def merged(parts):
@@ -133,13 +136,39 @@
 
 
 def sinkhorn_kernel(
-    info, got, group, plan, row_out, col_out, lse, tiles, row_in, row_all, col_in, col_all, sends, arrivals
+    info,
+    wants,
+    embed,
+    plan,
+    row_out,
+    col_out,
+    logits,
+    group,
+    got,
+    stage,
+    asked,
+    asked_smem,
+    lse,
+    tiles,
+    row_in,
+    row_all,
+    col_in,
+    col_all,
+    sends,
+    arrivals,
+    block_sends,
+    block_arrivals,
+    tile_sends,
+    tile_arrivals,
+    local,
 ):
     row_count = lax.axis_size("row")
     col_count = lax.axis_size("col")
     my_row = lax.axis_index("row")
     my_col = lax.axis_index("col")
-    width = got.shape[2]
+    width = group.shape[3]
+    share = CAP // col_count
+    ring = row_count // 2
     barrier = pltpu.get_barrier_semaphore()
 
     def greet(axis):
@@ -156,20 +185,116 @@
 
     greet("row")
     greet("col")
-
-    def logit(i, carry):
-        for k in range(4):
-            s = 4 * i + k
-            ah, al = split_two(got[info[2, s]])
-            bh, bl = split_two(group[info[1, s]])
+    group[my_row] = embed[1]
+
+    pl.semaphore_wait(barrier, row_count + col_count - 2)
+
+    def at(block, y_step, z_step):
+        z, y = block // ring, lax.rem(block, ring)
+        return lax.rem(z + z_step, 2) * ring + lax.rem(y + y_step + ring, ring)
+
+    half = TD // 2
+    whole, first, last = pl.ds(0, TD), pl.ds(0, half), pl.ds(half, half)
+    hops = (
+        (0, 1, 0, 0, whole),
+        (1, 0, 0, 0, whole),
+        (-1, 0, 0, 0, whole),
+        (1, 0, 0, 1, whole),
+        (-1, 0, 0, 1, whole),
+        (1, 0, -1, 0, first),
+        (-1, 0, 1, 0, last),
+        (1, 0, -1, 1, first),
+        (-1, 0, 1, 1, last),
+    )
+
+    def hop(n, landed):
+        peer_y, peer_z, block_y, block_z, part = hops[n]
+        block = at(my_row, block_y - (peer_y if landed else 0), block_z + (peer_z if landed else 0))
+        return pltpu.make_async_remote_copy(
+            src_ref=group.at[block, part],
+            dst_ref=group.at[block, part],
+            send_sem=block_sends.at[n],
+            recv_sem=block_arrivals.at[n],
+            device_id={"row": at(my_row, peer_y, peer_z)},
+            device_id_type=pl.DeviceIdType.MESH,
+        )
+
+    for n in range(3):
+        hop(n, False).start()
+
+    exchange(
+        4 * ITERS,
+        "col",
+        lambda peer: wants.at[peer],
+        lambda owner: asked.at[owner],
+        sends,
+        arrivals,
+    )
+    asked[my_col] = wants[my_col]
+    down = pltpu.make_async_copy(asked, asked_smem, local)
+    down.start()
+    down.wait()
+
+    def tiles_of(owner):
+        return pl.ds(owner * share, share)
+
+    def to_peer(d, landed):
+        peer = lax.rem(my_col + d, col_count)
+        return pltpu.make_async_remote_copy(
+            src_ref=stage.at[tiles_of(peer)],
+            dst_ref=got.at[tiles_of(landed)],
+            send_sem=tile_sends.at[d],
+            recv_sem=tile_arrivals.at[d],
+            device_id={"col": peer},
+            device_id_type=pl.DeviceIdType.MESH,
+        )
+
+    def send_tiles(d, carry):
+        peer = lax.rem(my_col + d, col_count)
+        for k in range(share):
+            stage[peer * share + k] = embed[0, asked_smem[peer, 0, k]]
+        to_peer(d, my_col).start()
+        return carry
+
+    lax.fori_loop(1, col_count, send_tiles, 0)
+    for k in range(share):
+        got[my_col * share + k] = embed[0, asked_smem[my_col, 0, k]]
+
+    for waited, started in ((1, (5,)), (2, (6,)), (0, (3, 4)), (3, (7,)), (4, (8,))):
+        hop(waited, True).wait_recv()
+        for n in started:
+            hop(n, False).start()
+    for n in range(5, 9):
+        hop(n, True).wait_recv()
+
+    def logit(owner):
+        for k in range(share):
+            x = owner * share + k
+            column = info[1, x]
+            ah, al = split_two(got[x])
+            bh, bl = split_two(group[column // TD, lax.rem(column, TD)])
             left = jnp.concatenate([ah, ah, al], axis=1)
             right = jnp.concatenate([bh, bl, bh], axis=1)
             both = lax.dot_general(left, right, (((1,), (1,)), ((), ())), preferred_element_type=F32)
-            plan[s] = both * (SHARPNESS / math.sqrt(width))
-        return carry
-
-    lax.fori_loop(0, CAP // 4, logit, 0)
-    pl.semaphore_wait(barrier, row_count + col_count - 2)
+            logits[x] = both * (SHARPNESS / math.sqrt(width))
+
+    logit(my_col)
+
+    def landed_tiles(d, carry):
+        owner = lax.rem(my_col - d + col_count, col_count)
+        to_peer(d, owner).wait_recv()
+        logit(owner)
+        return carry
+
+    lax.fori_loop(1, col_count, landed_tiles, 0)
+
+    def sent_tiles(d, carry):
+        to_peer(d, my_col).wait_send()
+        return carry
+
+    lax.fori_loop(1, col_count, sent_tiles, 0)
+    for n in range(9):
+        hop(n, False).wait_send()
 
     lanes = lax.broadcasted_iota(jnp.int32, (TILE, TILE), 1)
 
@@ -179,7 +304,7 @@
             sums = jnp.ones((TILE, TILE), F32)
             for k in range(8):
                 s = 8 * g + k
-                x = plan[s]
+                x = logits[s]
                 if it > 0:
                     x = x + col_all[it - 1, pl.ds(info[1, s], 1), :]
                 top = jnp.max(x, axis=1, keepdims=True)
@@ -191,17 +316,17 @@
 
         lax.fori_loop(0, CAP // 8, eight, 0)
 
-    def columns(it, g):
-        rows = [row_all[it, pl.ds(info[0, 8 * g + k], 1), :] for k in range(8)]
+    def columns(it, g, which):
+        rows = [row_all[it, pl.ds(info[which, 8 * g + k], 1), :] for k in range(8)]
         rows = jnp.concatenate(rows, axis=0)
         return jnp.transpose(jnp.concatenate([rows] * (TILE // 8), axis=0))
 
     def along_rows(it):
         def eight(g, carry):
-            pots = columns(it, g)
+            pots = columns(it, g, 0)
             tops, sums = [], []
             for k in range(8):
-                x = plan[8 * g + k] + pots[:, k : k + 1]
+                x = logits[8 * g + k] + pots[:, k : k + 1]
                 top = jnp.max(x, axis=0, keepdims=True)
                 tops.append(top)
                 sums.append(jnp.sum(jnp.exp(x - top), axis=0, keepdims=True))
@@ -266,20 +391,22 @@
     col_out[...] = col_all[ITERS - 1]
 
     def finish(g, carry):
-        pots = columns(ITERS - 1, g)
+        pots = columns(ITERS - 1, g, 6)
         for k in range(8):
             s = 8 * g + k
-            x = plan[s] + pots[:, k : k + 1] + col_all[ITERS - 1, pl.ds(info[1, s], 1), :]
+            x = logits[info[2, s]] + pots[:, k : k + 1] + col_all[ITERS - 1, pl.ds(info[7, s], 1), :]
             plan[s] = jnp.where(jnp.full((TILE, TILE), info[5, s], jnp.int32) > 0, x, 0.0)
         return carry
 
     lax.fori_loop(0, CAP // 8, finish, 0)
 
 
-def sinkhorn(info, got, group):
+def sinkhorn(info, wants, embed):
     row_count = lax.axis_size("row")
     col_count = lax.axis_size("col")
+    width = embed.shape[3]
     vmem = pl.BlockSpec(memory_space=pltpu.VMEM)
+    large = max(row_count, col_count)
     return pl.pallas_call(
         sinkhorn_kernel,
         in_specs=[pl.BlockSpec(memory_space=pltpu.SMEM), vmem, vmem],
@@ -290,20 +417,31 @@
             jax.ShapeDtypeStruct((TD * row_count, TILE), F32),
         ],
         scratch_shapes=[
+            pltpu.VMEM((CAP, TILE, TILE), F32),
+            pltpu.VMEM((row_count, TD, TILE, width), F32),
+            pltpu.VMEM((CAP, TILE, width), F32),
+            pltpu.VMEM((CAP, TILE, width), F32),
+            pltpu.VMEM((col_count, TD, TILE), jnp.int32),
+            pltpu.SMEM((col_count, TD, TILE), jnp.int32),
             pltpu.VMEM((CAP, TILE), F32),
-            pltpu.VMEM((TD * max(row_count, col_count), TILE), F32),
+            pltpu.VMEM((TD * large, TILE), F32),
             pltpu.VMEM((ITERS, col_count, TD, TILE), F32),
             pltpu.VMEM((ITERS, TD * col_count, TILE), F32),
             pltpu.VMEM((ITERS, row_count, TD, TILE), F32),
             pltpu.VMEM((ITERS, TD * row_count, TILE), F32),
-            pltpu.SemaphoreType.DMA((4 * ITERS, max(row_count, col_count))),
-            pltpu.SemaphoreType.DMA((4 * ITERS, max(row_count, col_count))),
+            pltpu.SemaphoreType.DMA((4 * ITERS + 1, large)),
+            pltpu.SemaphoreType.DMA((4 * ITERS + 1, large)),
+            pltpu.SemaphoreType.DMA((9,)),
+            pltpu.SemaphoreType.DMA((9,)),
+            pltpu.SemaphoreType.DMA((col_count,)),
+            pltpu.SemaphoreType.DMA((col_count,)),
+            pltpu.SemaphoreType.DMA,
         ],
         compiler_params=pltpu.CompilerParams(
-            collective_id=0, has_side_effects=True, vmem_limit_bytes=40 * 2**20
+            collective_id=0, has_side_effects=True, vmem_limit_bytes=48 * 2**20
         ),
         name="sinkhorn",
-    )(info, got, group)
+    )(info, wants, embed)
 
 
 def on_device(features, adj_vals, blk_cols, blk_count, send_list, weight, cand_tiles, cand_count):
@@ -316,17 +454,31 @@
     rows_here = cand_tiles[0, 0, 0]
     cols_here = cand_tiles[0, 0, 1]
     share = CAP // col_count
-    wanted = lax.all_gather(rows_here, "col")
-    part = wanted // TD
     slots = jnp.arange(CAP, dtype=jnp.int32)
     earlier = slots[None, :] < slots[:, None]
-    rank = jnp.sum((part[:, :, None] == part[:, None, :]) & earlier[None], axis=2, dtype=jnp.int32)
-    me = lax.axis_index("col")
-    hit = (part == me)[:, None, :] & (rank[:, None, :] == jnp.arange(share)[None, :, None])
-    asked = jnp.sum(jnp.where(hit, (wanted % TD)[:, None, :], 0), axis=2, dtype=jnp.int32)
-    my_part = rows_here // TD
-    my_rank = jnp.sum((my_part[:, None] == my_part[None, :]) & earlier, axis=1, dtype=jnp.int32)
-    place = jnp.clip(my_part * share + my_rank, 0, CAP - 1)
+    part = rows_here // TD
+    rank = jnp.sum((part[:, None] == part[None, :]) & earlier, axis=1, dtype=jnp.int32)
+    place = jnp.clip(part * share + rank, 0, CAP - 1)
+    live = (slots < cand_count[0, 0]).astype(jnp.int32)
+    hit = (place[:, None] == slots[None, :]).astype(jnp.int32)
+
+    def in_order(values):
+        return jnp.sum(hit * values[:, None], axis=0, dtype=jnp.int32)
+
+    info = jnp.stack(
+        [
+            in_order(rows_here),
+            in_order(cols_here),
+            place,
+            in_order(jnp.where(live > 0, rows_here, -1)),
+            in_order(jnp.where(live > 0, cols_here, -1)),
+            live,
+            rows_here,
+            cols_here,
+        ]
+    )
+    wants = (info[0] % TD).reshape(col_count, 1, share)
+    wants = jnp.pad(wants, ((0, 0), (0, TD - 1), (0, TILE - share)))
 
     picks = send_list[:, 0] + jnp.arange(2, dtype=jnp.int32)[:, None] * rows_dev
     per_dest = send_list.shape[2] // devices
@@ -335,23 +487,9 @@
     ghost = lax.all_to_all(outgoing, ("row", "col"), 0, 0, tiled=True)
     ghost = ghost.reshape(devices, 2, per_dest, width).transpose(1, 0, 2, 3).reshape(2, -1, width)
 
-    target = aggregate(features, ghost, adj_vals, blk_cols, blk_count[:, :], weight, 1)
-    target_group = lax.all_gather(target, "row", axis=0, tiled=True).reshape(-1, TILE, width)
-    source = aggregate(features, ghost, adj_vals, blk_cols, blk_count, weight, 0)
-    sent = source.reshape(TD, TILE, width)[asked.reshape(-1)].reshape(col_count, share * TILE, width)
-    got = lax.all_to_all(sent, "col", 0, 0, tiled=True).reshape(CAP, TILE, width)
-    live = slots < cand_count[0, 0]
-    info = jnp.stack(
-        [
-            rows_here,
-            cols_here,
-            place,
-            jnp.where(live, rows_here, -1),
-            jnp.where(live, cols_here, -1),
-            live.astype(jnp.int32),
-        ]
-    )
-    log_plan, row_pot, col_pot = sinkhorn(info, got, target_group)
+    embed = aggregate(features, ghost, adj_vals, blk_cols, blk_count, weight)
+    embed = embed.reshape(2, TD, TILE, width)
+    log_plan, row_pot, col_pot = sinkhorn(info, wants, embed)
     return (
         log_plan[None, None],
         row_pot.reshape(1, col_count, -1),

time: 317 us -> 266 us (0.84)
  waiting for transfers between devices: 145 us -> 18 us
  Pallas kernels: 94.5 us -> 216 us
  blocking collectives: 17 us -> 0 us
  between operations: 14.9 us -> 1.48 us
  local copies, waits for them, and re-layouts: 27.5 us -> 18.3 us
  starting transfers between devices: 15.8 us -> 11.1 us
    pallas_call x1, Pallas kernels: 66.4 us -> 194 us  [sinkhorn(): pl.pallas_call(sinkhorn_kernel, in_specs=[pl.BlockSpec(memory_space=pltpu...]
    all_to_all x1 -> x0, waiting for transfers between devices: 86.3 us -> none  [on_device(): lax.all_to_all(sent, 'col', 0, 0, tiled=True).reshape(CAP, TILE, width)]
    all_gather x1 -> x0, waiting for transfers between devices: 39.5 us -> none  [on_device(): lax.all_gather(target, 'row', axis=0, tiled=True).reshape(-1, TILE, width)]
    all_gather x1 -> x0, blocking collectives: 17 us -> none  [on_device(): wanted = lax.all_gather(rows_here, 'col')]
    pallas_call x2 -> x1, Pallas kernels: 28.1 us -> 21.5 us  [aggregate(): pl.pallas_call(aggregate_kernel, grid_spec=grid_spec, out_shape=jax.Shape...]
    unnamed x22 -> x14, local copies, waits for them, and re-layouts: 12.9 us -> 7.24 us
    all_to_all x1 -> x0, starting transfers between devices: 4.65 us -> none  [on_device(): lax.all_to_all(sent, 'col', 0, 0, tiled=True).reshape(CAP, TILE, width)]
    gather x1 -> x0, local copies, waits for them, and re-layouts: 3.53 us -> none  [on_device(): source.reshape(TD, TILE, width)[asked.reshape(-1)]]
  transfers between devices with their start and end apart: 3 -> 1, of which waited for: 3 -> 1; matrix products, arithmetic and copies ran while one was open for 1% -> 0% of each run, Pallas kernels for 5% -> 0%
where the time goes in v3:
time: 266 us
  Pallas kernels  216 us (81%)
  local copies, waits for them, and re-layouts  18.3 us (7%)
  waiting for transfers between devices  18 us (7%)
  starting transfers between devices  11.1 us (4%)
    pallas_call x1, Pallas kernels, sinkhorn(): pl.pallas_call(sinkhorn_kernel, in_specs=[pl.BlockSpec(memory_space=pltpu...  194 us
    pallas_call x1, Pallas kernels, aggregate(): pl.pallas_call(aggregate_kernel, grid_spec=grid_spec, out_shape=jax.Shape...  21.5 us
    all_to_all x1, waiting for transfers between devices, on_device(): ghost = lax.all_to_all(outgoing, ('row', 'col'), 0, 0, tiled=True)  18 us
    all_to_all x1, starting transfers between devices, on_device(): ghost = lax.all_to_all(outgoing, ('row', 'col'), 0, 0, tiled=True)  11.1 us
    unnamed x14, local copies, waits for them, and re-layouts  7.24 us
    gather x1, local copies, waits for them, and re-layouts, on_device(): features.reshape(2 * rows_dev, width)[picks]  6.27 us
  transfers between devices with their start and end apart: 1, of which 1 were waited for; matrix products, arithmetic and copies ran while one was open for 0% of the time, Pallas kernels for 0%

profile of v3, /device:TPU:0, one launch (start us, length us, event | category | flops | bytes accessed | tf_op | source)
XLA Modules:
  0.0 266.0 jit_solution(2669193640959868483)
XLA Ops:
  0.6 0.7 reduce
  1.3 0.1 squeeze.15
  1.5 0.1 add_bitcast_fusion
  1.6 0.1 copy.32
  1.7 0.2 reshape.288
  1.9 0.0 copy-start.5
  1.9 6.3 %gather_fusion = f32[1024,256]{1,0:T(8,128)} fusion(f32[2048,256]{1,0:T(8,128)} %bitcast.39, s32[1024]{0:T(1024)S(1)} %broadcast_clamp_fusion), kind=kCustom, calls=%fused_computation | custom fusion | bytes 2101248 | tf_op jit(solution)/shard_map/gather | solution.py:486
  8.2 11.1 %all-to-all-start = ((f32[128,8,256]{2,1,0:T(8,128)}), f32[128,8,256]{2,1,0:T(8,128)S(1)}, u32[]{:S(2)}, u32[]{:S(2)}) async-start(f32[128,8,256]{2,1,0:T(8,128)} %bitcast.14), calls=%async_computation | async-start | bytes 2097152 | tf_op jit(solution)/shard_map/all_to_all | solution.py:487
  20.0 0.0 copy-done.5
  20.0 0.2 convert_reduce_fusion
  20.2 0.1 select_reduce_fusion
  20.3 0.1 reduce_sum.55
  20.5 0.0 copy-start
  20.6 0.0 copy-start.3
  20.6 0.0 copy-start.4
  20.6 18.0 %all-to-all-done = f32[128,8,256]{2,1,0:T(8,128)S(1)} async-done(((f32[128,8,256]{2,1,0:T(8,128)}), f32[128,8,256]{2,1,0:T(8,128)S(1)}, u32[]{:S(2)}, u32[]{:S(2)}) %all-to-all-start) | async-done | bytes 1048608 | tf_op jit(solution)/shard_map/all_to_all | solution.py:487
  38.5 0.3 copy.33
  38.9 1.6 copy.34
  40.5 1.6 reshape.291.ghost_ref
  42.1 0.0 copy-done
  42.1 0.0 copy-done.3
  42.1 0.0 copy-done.4
  42.1 0.0 copy-start.1
  42.2 4.0 %copy-done.1 = bf16[2,8,20,128,128]{4,3,2,1,0:T(8,128)(2,1)S(1)} copy-done((bf16[2,8,20,128,128]{4,3,2,1,0:T(8,128)(2,1)S(1)}, bf16[2,8,20,128,128]{4,3,2,1,0:T(8,128)(2,1)}, u32[]{:S(2)}) %copy-start.1) | copy-done | bytes 10485784
  46.1 0.0 copy-start.2
  46.2 0.9 copy-done.2
  47.1 21.5 %aggregate.1 = f32[2,1024,256]{2,1,0:T(8,128)S(1)} custom-call(s32[2,8,20]{2,1,0:T(8,128)S(1)} %copy-done.3, s32[2,8]{1,0:T(2,128)S(1)} %copy-done.4, bf16[2,8,20,128,128]{4,3,2,1,0:T(8,128)(2,1)S(1)} %copy-done.1, f32[2,1024,256]{2,1,0:T(8,128)S(1)} %copy-done, f32[2,512,256]{2,1,0:T(8,128)S(1)} %reshape.291.ghost_ref, f32[256,256]{1,0:T(8,128)S(1)} %copy-done.2), custom_call_target="tpu_custom_call" | custom-call | flops 5368709120 | bytes 16777216 | tf_op jit(solution)/shard_map/aggregate/pallas_call | solution.py:91
  68.6 194.5 %sinkhorn.1 = (f32[48,128,128]{2,1,0:T(8,128)S(1)}, f32[128,128]{1,0:T(8,128)S(1)}, f32[64,128]{1,0:T(8,128)S(1)}) custom-call(s32[8,48]{1,0:T(8,128)S(1)} %stack.21.info, s32[16,8,128]{2,1,0:T(8,128)S(1)} %pad.4.wants, f32[2,8,128,256]{3,2,1,0:T(8,128)S(1)} %bitcast.41), custom_call_target="tpu_custom_call" | custom-call | tf_op jit(solution)/shard_map/sinkhorn/pallas_call | solution.py:410
  263.1 0.6 reshape.293
  263.7 1.7 copy.39
  265.4 0.6 copy.40
  (11 shorter events, 0.1 us)
Async XLA Ops:
  1.9 18.1 %copy-start.5 = (s32[1,1,2,48]{3,2,1,0:T(2,128)S(1)}, s32[1,1,2,48]{3,2,1,0:T(2,128)}, u32[]{:S(2)}) copy-start(s32[1,1,2,48]{3,2,1,0:T(2,128)} %param.14) | copy-start | bytes 1156
  8.2 30.3 %all-to-all-start = ((f32[128,8,256]{2,1,0:T(8,128)}), f32[128,8,256]{2,1,0:T(8,128)S(1)}, u32[]{:S(2)}, u32[]{:S(2)}) async-start(f32[128,8,256]{2,1,0:T(8,128)} %bitcast.14), calls=%async_computation | async-start | bytes 2097152 | tf_op jit(solution)/shard_map/all_to_all | solution.py:487
  20.5 21.6 %copy-start = (f32[2,1024,256]{2,1,0:T(8,128)S(1)}, f32[2,1024,256]{2,1,0:T(8,128)}, u32[]{:S(2)}) copy-start(f32[2,1024,256]{2,1,0:T(8,128)} %own_ref.1) | copy-start | bytes 6291460
  20.6 21.6 %copy-start.3 = (s32[2,8,20]{2,1,0:T(8,128)S(1)}, s32[2,8,20]{2,1,0:T(8,128)}, u32[]{:S(2)}) copy-start(s32[2,8,20]{2,1,0:T(8,128)} %cols.1) | copy-start | bytes 3844
  20.6 21.6 %copy-start.4 = (s32[2,8]{1,0:T(2,128)S(1)}, s32[2,8]{1,0:T(2,128)}, u32[]{:S(2)}) copy-start(s32[2,8]{1,0:T(2,128)} %count.1) | copy-start | bytes 196
  42.1 4.0 %copy-start.1 = (bf16[2,8,20,128,128]{4,3,2,1,0:T(8,128)(2,1)S(1)}, bf16[2,8,20,128,128]{4,3,2,1,0:T(8,128)(2,1)}, u32[]{:S(2)}) copy-start(bf16[2,8,20,128,128]{4,3,2,1,0:T(8,128)(2,1)} %adj_ref.1) | copy-start | bytes 31457284
  46.1 0.9 copy-start.2

commit v4 on v2

--- a/solution.py
+++ b/solution.py
@@ -23,7 +23,8 @@
 
 
 def aggregate_kernel(cols, count, adj_ref, own_ref, ghost_ref, weight_ref, out_ref, table, wstack, acc, deg):
-    t = pl.program_id(0)
+    g = pl.program_id(0)
+    t = pl.program_id(1)
     own_rows, width = own_ref.shape
 
     @pl.when(t == 0)
@@ -43,15 +44,15 @@
 
     acc[...] = jnp.zeros_like(acc)
     deg[...] = jnp.zeros_like(deg)
-    n = count[t]
+    n = count[g, t]
 
     def pair(i, carry):
         b = 2 * i
         first = adj_ref[0, b]
         second = adj_ref[0, b + 1]
         second = jnp.where(b + 1 < n, second, jnp.zeros_like(second))
-        one = table[pl.ds(pl.multiple_of(cols[t, b] * TILE, TILE), TILE), :]
-        two = table[pl.ds(pl.multiple_of(cols[t, b + 1] * TILE, TILE), TILE), :]
+        one = table[pl.ds(pl.multiple_of(cols[g, t, b] * TILE, TILE), TILE), :]
+        two = table[pl.ds(pl.multiple_of(cols[g, t, b + 1] * TILE, TILE), TILE), :]
         left = jnp.concatenate([first, second], axis=1)
         right = jnp.concatenate([one, two], axis=0)
         acc[...] += jnp.dot(left, right, preferred_element_type=F32)
@@ -67,19 +68,19 @@
     out_ref[...] = own + jnp.maximum(mixed, 0.0)
 
 
-def aggregate(own, ghost, adj, cols, count, weight, graph):
-    rows, width = own.shape[1:]
+def aggregate(own, ghost, adj, cols, count, weight):
+    graphs, rows, width = own.shape
     tiles, blocks = adj.shape[1:3]
     grid_spec = pltpu.PrefetchScalarGridSpec(
         num_scalar_prefetch=2,
-        grid=(tiles,),
+        grid=(graphs, tiles),
         in_specs=[
-            pl.BlockSpec((None, 1, blocks, TILE, TILE), lambda t, *_: (graph, t, 0, 0, 0)),
-            pl.BlockSpec((None, rows, width), lambda t, *_: (graph, 0, 0)),
-            pl.BlockSpec((None, ghost.shape[1], width), lambda t, *_: (graph, 0, 0)),
-            pl.BlockSpec((width, width), lambda t, *_: (0, 0)),
+            pl.BlockSpec((None, 1, blocks, TILE, TILE), lambda g, t, *_: (g, t, 0, 0, 0)),
+            pl.BlockSpec((None, rows, width), lambda g, t, *_: (g, 0, 0)),
+            pl.BlockSpec((None, ghost.shape[1], width), lambda g, t, *_: (g, 0, 0)),
+            pl.BlockSpec((width, width), lambda g, t, *_: (0, 0)),
         ],
-        out_specs=pl.BlockSpec((TILE, width), lambda t, *_: (t, 0)),
+        out_specs=pl.BlockSpec((None, TILE, width), lambda g, t, *_: (g, t, 0)),
         scratch_shapes=[
             pltpu.VMEM((rows + ghost.shape[1], 2 * width), BF16),
             pltpu.VMEM((3 * width, width), BF16),
@@ -90,13 +91,15 @@
     return pl.pallas_call(
         aggregate_kernel,
         grid_spec=grid_spec,
-        out_shape=jax.ShapeDtypeStruct((rows, width), F32),
+        out_shape=jax.ShapeDtypeStruct((graphs, rows, width), F32),
         compiler_params=pltpu.CompilerParams(vmem_limit_bytes=24 * 2**20),
         cost_estimate=pl.CostEstimate(
-            flops=tiles * blocks * TILE * TILE * width * 4, bytes_accessed=8 * 2**20, transcendentals=0
+            flops=graphs * tiles * blocks * TILE * TILE * width * 4,
+            bytes_accessed=16 * 2**20,
+            transcendentals=0,
         ),
         name="aggregate",
-    )(cols[graph], count[graph], adj, own, ghost, weight)
+    )(cols, count, adj, own, ghost, weight)
 
 
 def merged(parts):
@@ -133,13 +136,35 @@
 
 
 def sinkhorn_kernel(
-    info, got, group, plan, row_out, col_out, lse, tiles, row_in, row_all, col_in, col_all, sends, arrivals
+    info,
+    embed,
+    plan,
+    row_out,
+    col_out,
+    sources,
+    targets,
+    lse,
+    tiles,
+    row_in,
+    row_all,
+    col_in,
+    col_all,
+    sends,
+    arrivals,
+    row_sends,
+    row_arrivals,
+    col_sends,
+    col_arrivals,
+    twin_sends,
+    twin_arrivals,
 ):
     row_count = lax.axis_size("row")
     col_count = lax.axis_size("col")
     my_row = lax.axis_index("row")
     my_col = lax.axis_index("col")
-    width = got.shape[2]
+    width = embed.shape[3]
+    ring = row_count // 2
+    span = col_count // 4
     barrier = pltpu.get_barrier_semaphore()
 
     def greet(axis):
@@ -156,12 +181,95 @@
 
     greet("row")
     greet("col")
+    sources[my_col] = embed[0]
+    targets[my_row] = embed[1]
+
+    pl.semaphore_wait(barrier, row_count + col_count - 2)
+
+    def at_row(block, step, across):
+        z, y = block // ring, lax.rem(block, ring)
+        return lax.rem(z + across, 2) * ring + lax.rem(y + step + ring, ring)
+
+    def at_col(block, step, across):
+        core = lax.rem(block, 2)
+        z, x = block // (2 * span), lax.rem(block // 2, span)
+        return (lax.rem(z + across, 2) * span + lax.rem(x + step + span, span)) * 2 + core
+
+    half = TD // 2
+    whole, first, last = pl.ds(0, TD), pl.ds(0, half), pl.ds(half, half)
+    hops = (
+        (0, 1, 0, 0, whole),
+        (1, 0, 0, 0, whole),
+        (-1, 0, 0, 0, whole),
+        (1, 0, 0, 1, whole),
+        (-1, 0, 0, 1, whole),
+        (1, 0, -1, 0, first),
+        (-1, 0, 1, 0, last),
+        (1, 0, -1, 1, first),
+        (-1, 0, 1, 1, last),
+    )
+
+    def hop(axis, n, landed):
+        at, me, blocks, sent, arrived = (
+            (at_row, my_row, targets, row_sends, row_arrivals)
+            if axis == "row"
+            else (at_col, my_col, sources, col_sends, col_arrivals)
+        )
+        step, across, block_step, block_across, part = hops[n]
+        if landed:
+            block_step, block_across = block_step - step, block_across + across
+        block = at(me, block_step, block_across)
+        return pltpu.make_async_remote_copy(
+            src_ref=blocks.at[block, part],
+            dst_ref=blocks.at[block, part],
+            send_sem=sent.at[n],
+            recv_sem=arrived.at[n],
+            device_id={axis: at(me, step, across)},
+            device_id_type=pl.DeviceIdType.MESH,
+        )
+
+    twin = my_col + 1 - 2 * lax.rem(my_col, 2)
+
+    def pass_on(n, landed):
+        owner = twin if landed else my_col
+        block, part = owner, whole
+        if n > 0:
+            step, across, block_step, block_across, part = hops[n - 1]
+            block = at_col(owner, block_step - step, block_across + across)
+        return pltpu.make_async_remote_copy(
+            src_ref=sources.at[block, part],
+            dst_ref=sources.at[block, part],
+            send_sem=twin_sends.at[n],
+            recv_sem=twin_arrivals.at[n],
+            device_id={"col": twin},
+            device_id_type=pl.DeviceIdType.MESH,
+        )
+
+    for n in range(3):
+        hop("row", n, False).start()
+        hop("col", n, False).start()
+    pass_on(0, False).start()
+    follow = {1: (5,), 2: (6,), 0: (3, 4), 3: (7,), 4: (8,)}
+    for n in (1, 2, 0, 3, 4, 5, 6, 7, 8):
+        for axis in ("row", "col"):
+            hop(axis, n, True).wait_recv()
+            for later in follow.get(n, ()):
+                hop(axis, later, False).start()
+        pass_on(n + 1, False).start()
+    for n in range(10):
+        pass_on(n, True).wait_recv()
+    for n in range(10):
+        pass_on(n, False).wait_send()
+    for n in range(9):
+        hop("row", n, False).wait_send()
+        hop("col", n, False).wait_send()
 
     def logit(i, carry):
         for k in range(4):
             s = 4 * i + k
-            ah, al = split_two(got[info[2, s]])
-            bh, bl = split_two(group[info[1, s]])
+            row, column = info[0, s], info[1, s]
+            ah, al = split_two(sources[row // TD, lax.rem(row, TD)])
+            bh, bl = split_two(targets[column // TD, lax.rem(column, TD)])
             left = jnp.concatenate([ah, ah, al], axis=1)
             right = jnp.concatenate([bh, bl, bh], axis=1)
             both = lax.dot_general(left, right, (((1,), (1,)), ((), ())), preferred_element_type=F32)
@@ -169,7 +277,6 @@
         return carry
 
     lax.fori_loop(0, CAP // 4, logit, 0)
-    pl.semaphore_wait(barrier, row_count + col_count - 2)
 
     lanes = lax.broadcasted_iota(jnp.int32, (TILE, TILE), 1)
 
@@ -270,19 +377,21 @@
         for k in range(8):
             s = 8 * g + k
             x = plan[s] + pots[:, k : k + 1] + col_all[ITERS - 1, pl.ds(info[1, s], 1), :]
-            plan[s] = jnp.where(jnp.full((TILE, TILE), info[5, s], jnp.int32) > 0, x, 0.0)
+            plan[s] = jnp.where(jnp.full((TILE, TILE), info[2, s], jnp.int32) > 0, x, 0.0)
         return carry
 
     lax.fori_loop(0, CAP // 8, finish, 0)
 
 
-def sinkhorn(info, got, group):
+def sinkhorn(info, embed):
     row_count = lax.axis_size("row")
     col_count = lax.axis_size("col")
+    width = embed.shape[3]
     vmem = pl.BlockSpec(memory_space=pltpu.VMEM)
+    large = max(row_count, col_count)
     return pl.pallas_call(
         sinkhorn_kernel,
-        in_specs=[pl.BlockSpec(memory_space=pltpu.SMEM), vmem, vmem],
+        in_specs=[pl.BlockSpec(memory_space=pltpu.SMEM), vmem],
         out_specs=[vmem] * 3,
         out_shape=[
             jax.ShapeDtypeStruct((CAP, TILE, TILE), F32),
@@ -290,20 +399,28 @@
             jax.ShapeDtypeStruct((TD * row_count, TILE), F32),
         ],
         scratch_shapes=[
+            pltpu.VMEM((col_count, TD, TILE, width), F32),
+            pltpu.VMEM((row_count, TD, TILE, width), F32),
             pltpu.VMEM((CAP, TILE), F32),
-            pltpu.VMEM((TD * max(row_count, col_count), TILE), F32),
+            pltpu.VMEM((TD * large, TILE), F32),
             pltpu.VMEM((ITERS, col_count, TD, TILE), F32),
             pltpu.VMEM((ITERS, TD * col_count, TILE), F32),
             pltpu.VMEM((ITERS, row_count, TD, TILE), F32),
             pltpu.VMEM((ITERS, TD * row_count, TILE), F32),
-            pltpu.SemaphoreType.DMA((4 * ITERS, max(row_count, col_count))),
-            pltpu.SemaphoreType.DMA((4 * ITERS, max(row_count, col_count))),
+            pltpu.SemaphoreType.DMA((4 * ITERS, large)),
+            pltpu.SemaphoreType.DMA((4 * ITERS, large)),
+            pltpu.SemaphoreType.DMA((9,)),
+            pltpu.SemaphoreType.DMA((9,)),
+            pltpu.SemaphoreType.DMA((9,)),
+            pltpu.SemaphoreType.DMA((9,)),
+            pltpu.SemaphoreType.DMA((10,)),
+            pltpu.SemaphoreType.DMA((10,)),
         ],
         compiler_params=pltpu.CompilerParams(
-            collective_id=0, has_side_effects=True, vmem_limit_bytes=40 * 2**20
+            collective_id=0, has_side_effects=True, vmem_limit_bytes=48 * 2**20
         ),
         name="sinkhorn",
-    )(info, got, group)
+    )(info, embed)
 
 
 def on_device(features, adj_vals, blk_cols, blk_count, send_list, weight, cand_tiles, cand_count):
@@ -315,19 +432,16 @@
 
     rows_here = cand_tiles[0, 0, 0]
     cols_here = cand_tiles[0, 0, 1]
-    share = CAP // col_count
-    wanted = lax.all_gather(rows_here, "col")
-    part = wanted // TD
-    slots = jnp.arange(CAP, dtype=jnp.int32)
-    earlier = slots[None, :] < slots[:, None]
-    rank = jnp.sum((part[:, :, None] == part[:, None, :]) & earlier[None], axis=2, dtype=jnp.int32)
-    me = lax.axis_index("col")
-    hit = (part == me)[:, None, :] & (rank[:, None, :] == jnp.arange(share)[None, :, None])
-    asked = jnp.sum(jnp.where(hit, (wanted % TD)[:, None, :], 0), axis=2, dtype=jnp.int32)
-    my_part = rows_here // TD
-    my_rank = jnp.sum((my_part[:, None] == my_part[None, :]) & earlier, axis=1, dtype=jnp.int32)
-    place = jnp.clip(my_part * share + my_rank, 0, CAP - 1)
-
+    live = jnp.arange(CAP, dtype=jnp.int32) < cand_count[0, 0]
+    info = jnp.stack(
+        [
+            rows_here,
+            cols_here,
+            live.astype(jnp.int32),
+            jnp.where(live, rows_here, -1),
+            jnp.where(live, cols_here, -1),
+        ]
+    )
     picks = send_list[:, 0] + jnp.arange(2, dtype=jnp.int32)[:, None] * rows_dev
     per_dest = send_list.shape[2] // devices
     picks = picks.reshape(2, devices, per_dest).transpose(1, 0, 2).reshape(-1)
@@ -335,23 +449,9 @@
     ghost = lax.all_to_all(outgoing, ("row", "col"), 0, 0, tiled=True)
     ghost = ghost.reshape(devices, 2, per_dest, width).transpose(1, 0, 2, 3).reshape(2, -1, width)
 
-    target = aggregate(features, ghost, adj_vals, blk_cols, blk_count[:, :], weight, 1)
-    target_group = lax.all_gather(target, "row", axis=0, tiled=True).reshape(-1, TILE, width)
-    source = aggregate(features, ghost, adj_vals, blk_cols, blk_count, weight, 0)
-    sent = source.reshape(TD, TILE, width)[asked.reshape(-1)].reshape(col_count, share * TILE, width)
-    got = lax.all_to_all(sent, "col", 0, 0, tiled=True).reshape(CAP, TILE, width)
-    live = slots < cand_count[0, 0]
-    info = jnp.stack(
-        [
-            rows_here,
-            cols_here,
-            place,
-            jnp.where(live, rows_here, -1),
-            jnp.where(live, cols_here, -1),
-            live.astype(jnp.int32),
-        ]
-    )
-    log_plan, row_pot, col_pot = sinkhorn(info, got, target_group)
+    embed = aggregate(features, ghost, adj_vals, blk_cols, blk_count, weight)
+    embed = embed.reshape(2, TD, TILE, width)
+    log_plan, row_pot, col_pot = sinkhorn(info, embed)
     return (
         log_plan[None, None],
         row_pot.reshape(1, col_count, -1),

time: 317 us -> 227 us (0.72)
  waiting for transfers between devices: 145 us -> 18.4 us
  Pallas kernels: 94.5 us -> 177 us
  blocking collectives: 17 us -> 0 us
  between operations: 14.9 us -> 1.46 us
  local copies, waits for them, and re-layouts: 27.5 us -> 17.3 us
  starting transfers between devices: 15.8 us -> 11.1 us
    all_to_all x1 -> x0, waiting for transfers between devices: 86.3 us -> none  [on_device(): lax.all_to_all(sent, 'col', 0, 0, tiled=True).reshape(CAP, TILE, width)]
    pallas_call x1, Pallas kernels: 66.4 us -> 152 us  [sinkhorn(): pl.pallas_call(sinkhorn_kernel, in_specs=[pl.BlockSpec(memory_space=pltpu...]
    all_gather x1 -> x0, waiting for transfers between devices: 39.5 us -> none  [on_device(): lax.all_gather(target, 'row', axis=0, tiled=True).reshape(-1, TILE, width)]
    all_gather x1 -> x0, blocking collectives: 17 us -> none  [on_device(): wanted = lax.all_gather(rows_here, 'col')]
    unnamed x22 -> x14, local copies, waits for them, and re-layouts: 12.9 us -> 6.3 us
    all_to_all x1 -> x0, starting transfers between devices: 4.65 us -> none  [on_device(): lax.all_to_all(sent, 'col', 0, 0, tiled=True).reshape(CAP, TILE, width)]
    gather x1 -> x0, local copies, waits for them, and re-layouts: 3.53 us -> none  [on_device(): source.reshape(TD, TILE, width)[asked.reshape(-1)]]
    pallas_call x2 -> x1, Pallas kernels: 28.1 us -> 25.4 us  [aggregate(): pl.pallas_call(aggregate_kernel, grid_spec=grid_spec, out_shape=jax.Shape...]
  transfers between devices with their start and end apart: 3 -> 1, of which waited for: 3 -> 1; matrix products, arithmetic and copies ran while one was open for 1% -> 0% of each run, Pallas kernels for 5% -> 0%
where the time goes in v4:
time: 227 us; the launch traced here: 226 us
  Pallas kernels  177 us (78%)
  waiting for transfers between devices  18.4 us (8%)
  local copies, waits for them, and re-layouts  17.3 us (8%)
  starting transfers between devices  11.1 us (5%)
    pallas_call x1, Pallas kernels, sinkhorn(): pl.pallas_call(sinkhorn_kernel, in_specs=[pl.BlockSpec(memory_space=pltpu...  152 us
    pallas_call x1, Pallas kernels, aggregate(): pl.pallas_call(aggregate_kernel, grid_spec=grid_spec, out_shape=jax.Shape...  25.4 us
    all_to_all x1, waiting for transfers between devices, on_device(): ghost = lax.all_to_all(outgoing, ('row', 'col'), 0, 0, tiled=True)  18.4 us
    all_to_all x1, starting transfers between devices, on_device(): ghost = lax.all_to_all(outgoing, ('row', 'col'), 0, 0, tiled=True)  11.1 us
    unnamed x14, local copies, waits for them, and re-layouts  6.3 us
    gather x1, local copies, waits for them, and re-layouts, on_device(): features.reshape(2 * rows_dev, width)[picks]  6.27 us
  transfers between devices with their start and end apart: 1, of which 1 were waited for; matrix products, arithmetic and copies ran while one was open for 0% of the time, Pallas kernels for 0%

profile of v4, /device:TPU:0, one launch (start us, length us, event | category | flops | bytes accessed | tf_op | source)
XLA Modules:
  0.0 226.4 jit_solution(17431802948146871090)
XLA Ops:
  0.6 0.7 reduce
  1.3 0.1 squeeze.9
  1.5 0.1 add_bitcast_fusion
  1.6 0.1 copy.16
  1.7 0.2 reshape.103
  1.9 0.0 copy-start.5
  1.9 6.3 %gather_fusion = f32[1024,256]{1,0:T(8,128)} fusion(f32[2048,256]{1,0:T(8,128)} %bitcast.22, s32[1024]{0:T(1024)S(1)} %broadcast_clamp_fusion), kind=kCustom, calls=%fused_computation | custom fusion | bytes 2101248 | tf_op jit(solution)/shard_map/gather | solution.py:448
  8.2 11.1 %all-to-all-start = ((f32[128,8,256]{2,1,0:T(8,128)}), f32[128,8,256]{2,1,0:T(8,128)S(1)}, u32[]{:S(2)}, u32[]{:S(2)}) async-start(f32[128,8,256]{2,1,0:T(8,128)} %bitcast.6), calls=%async_computation | async-start | bytes 2097152 | tf_op jit(solution)/shard_map/all_to_all | solution.py:449
  20.0 0.0 copy-done.5
  20.1 0.0 copy-start
  20.1 0.0 copy-start.2
  20.1 0.0 copy-start.3
  20.1 0.0 copy-start.4
  20.1 18.4 %all-to-all-done = f32[128,8,256]{2,1,0:T(8,128)S(1)} async-done(((f32[128,8,256]{2,1,0:T(8,128)}), f32[128,8,256]{2,1,0:T(8,128)S(1)}, u32[]{:S(2)}, u32[]{:S(2)}) %all-to-all-start) | async-done | bytes 1048608 | tf_op jit(solution)/shard_map/all_to_all | solution.py:449
  38.5 0.3 copy.17
  38.9 1.6 copy.18
  40.5 1.6 reshape.106.ghost_ref
  42.1 0.0 copy-done
  42.1 0.0 copy-done.2
  42.1 0.0 copy-done.3
  42.1 0.0 copy-done.4
  42.2 0.0 copy-start.1
  42.2 4.0 %copy-done.1 = bf16[2,8,20,128,128]{4,3,2,1,0:T(8,128)(2,1)S(1)} copy-done((bf16[2,8,20,128,128]{4,3,2,1,0:T(8,128)(2,1)S(1)}, bf16[2,8,20,128,128]{4,3,2,1,0:T(8,128)(2,1)}, u32[]{:S(2)}) %copy-start.1) | copy-done | bytes 10485784
  46.2 25.4 %aggregate.1 = f32[2,1024,256]{2,1,0:T(8,128)S(1)} custom-call(s32[2,8,20]{2,1,0:T(8,128)S(1)} %copy-done.3, s32[2,8]{1,0:T(2,128)S(1)} %copy-done.4, bf16[2,8,20,128,128]{4,3,2,1,0:T(8,128)(2,1)S(1)} %copy-done.1, f32[2,1024,256]{2,1,0:T(8,128)S(1)} %copy-done, f32[2,512,256]{2,1,0:T(8,128)S(1)} %reshape.106.ghost_ref, f32[256,256]{1,0:T(8,128)S(1)} %copy-done.2), custom_call_target="tpu_custom_call" | custom-call | flops 5368709120 | bytes 16777216 | tf_op jit(solution)/shard_map/aggregate/pallas_call | solution.py:91
  71.5 152.0 %sinkhorn.1 = (f32[48,128,128]{2,1,0:T(8,128)S(1)}, f32[128,128]{1,0:T(8,128)S(1)}, f32[64,128]{1,0:T(8,128)S(1)}) custom-call(s32[5,48]{1,0:T(8,128)S(1)} %stack.2.info, f32[2,8,128,256]{3,2,1,0:T(8,128)S(1)} %bitcast.24), custom_call_target="tpu_custom_call" | custom-call | tf_op jit(solution)/shard_map/sinkhorn/pallas_call | solution.py:392
  223.5 0.6 reshape.108
  224.2 1.7 copy.23
  225.8 0.6 copy.24
  (7 shorter events, 0.1 us)
Async XLA Ops:
  1.9 18.1 %copy-start.5 = (s32[1,1,2,48]{3,2,1,0:T(2,128)S(1)}, s32[1,1,2,48]{3,2,1,0:T(2,128)}, u32[]{:S(2)}) copy-start(s32[1,1,2,48]{3,2,1,0:T(2,128)} %param.14) | copy-start | bytes 1156
  8.2 30.3 %all-to-all-start = ((f32[128,8,256]{2,1,0:T(8,128)}), f32[128,8,256]{2,1,0:T(8,128)S(1)}, u32[]{:S(2)}, u32[]{:S(2)}) async-start(f32[128,8,256]{2,1,0:T(8,128)} %bitcast.6), calls=%async_computation | async-start | bytes 2097152 | tf_op jit(solution)/shard_map/all_to_all | solution.py:449
  20.1 22.0 %copy-start = (f32[2,1024,256]{2,1,0:T(8,128)S(1)}, f32[2,1024,256]{2,1,0:T(8,128)}, u32[]{:S(2)}) copy-start(f32[2,1024,256]{2,1,0:T(8,128)} %own_ref.1) | copy-start | bytes 6291460
  20.1 22.0 %copy-start.2 = (f32[256,256]{1,0:T(8,128)S(1)}, f32[256,256]{1,0:T(8,128)}, u32[]{:S(2)}) copy-start(f32[256,256]{1,0:T(8,128)} %weight_ref.1) | copy-start | bytes 786436
  20.1 22.0 %copy-start.3 = (s32[2,8,20]{2,1,0:T(8,128)S(1)}, s32[2,8,20]{2,1,0:T(8,128)}, u32[]{:S(2)}) copy-start(s32[2,8,20]{2,1,0:T(8,128)} %cols.1) | copy-start | bytes 3844
  20.1 22.0 %copy-start.4 = (s32[2,8]{1,0:T(2,128)S(1)}, s32[2,8]{1,0:T(2,128)}, u32[]{:S(2)}) copy-start(s32[2,8]{1,0:T(2,128)} %count.1) | copy-start | bytes 196
  42.2 4.0 %copy-start.1 = (bf16[2,8,20,128,128]{4,3,2,1,0:T(8,128)(2,1)S(1)}, bf16[2,8,20,128,128]{4,3,2,1,0:T(8,128)(2,1)}, u32[]{:S(2)}) copy-start(bf16[2,8,20,128,128]{4,3,2,1,0:T(8,128)(2,1)} %adj_ref.1) | copy-start | bytes 31457284

commit v5 on v4

--- a/solution.py
+++ b/solution.py
@@ -33,10 +33,19 @@
             hi, lo = split_two(own_ref[start : start + 256])
             table[start : start + 256, :width] = hi
             table[start : start + 256, width:] = lo
-        for start in range(0, ghost_ref.shape[0], 256):
-            hi, lo = split_two(ghost_ref[start : start + 256])
-            table[own_rows + start : own_rows + start + 256, :width] = hi
-            table[own_rows + start : own_rows + start + 256, width:] = lo
+        each = ghost_ref.shape[1] // 2
+
+        def repack(i, carry):
+            sent = [ghost_ref[4 * i + k] for k in range(4)]
+            upper = jnp.concatenate([piece[:each] for piece in sent], axis=0)
+            lower = jnp.concatenate([piece[each:] for piece in sent], axis=0)
+            hi, lo = split_two(jnp.where(g == 0, upper, lower))
+            rows = pl.ds(pl.multiple_of(own_rows + 4 * each * i, 4 * each), 4 * each)
+            table[rows, :width] = hi
+            table[rows, width:] = lo
+            return carry
+
+        lax.fori_loop(0, ghost_ref.shape[0] // 4, repack, 0)
         hi, lo = split_two(weight_ref[...])
         wstack[:width] = hi
         wstack[width : 2 * width] = lo
@@ -77,12 +86,12 @@
         in_specs=[
             pl.BlockSpec((None, 1, blocks, TILE, TILE), lambda g, t, *_: (g, t, 0, 0, 0)),
             pl.BlockSpec((None, rows, width), lambda g, t, *_: (g, 0, 0)),
-            pl.BlockSpec((None, ghost.shape[1], width), lambda g, t, *_: (g, 0, 0)),
+            pl.BlockSpec(ghost.shape, lambda g, t, *_: (0, 0, 0)),
             pl.BlockSpec((width, width), lambda g, t, *_: (0, 0)),
         ],
         out_specs=pl.BlockSpec((None, TILE, width), lambda g, t, *_: (g, t, 0)),
         scratch_shapes=[
-            pltpu.VMEM((rows + ghost.shape[1], 2 * width), BF16),
+            pltpu.VMEM((rows + ghost.shape[0] * ghost.shape[1] // 2, 2 * width), BF16),
             pltpu.VMEM((3 * width, width), BF16),
             pltpu.VMEM((TILE, 2 * width), F32),
             pltpu.VMEM((TILE, TILE), F32),
@@ -92,7 +101,7 @@
         aggregate_kernel,
         grid_spec=grid_spec,
         out_shape=jax.ShapeDtypeStruct((graphs, rows, width), F32),
-        compiler_params=pltpu.CompilerParams(vmem_limit_bytes=24 * 2**20),
+        compiler_params=pltpu.CompilerParams(vmem_limit_bytes=52 * 2**20),
         cost_estimate=pl.CostEstimate(
             flops=graphs * tiles * blocks * TILE * TILE * width * 4,
             bytes_accessed=16 * 2**20,
@@ -195,19 +204,21 @@
         z, x = block // (2 * span), lax.rem(block // 2, span)
         return (lax.rem(z + across, 2) * span + lax.rem(x + step + span, span)) * 2 + core
 
-    half = TD // 2
+    half, quarter = TD // 2, TD // 4
     whole, first, last = pl.ds(0, TD), pl.ds(0, half), pl.ds(half, half)
+    parts = [pl.ds(p * quarter, quarter) for p in range(4)]
     hops = (
-        (0, 1, 0, 0, whole),
-        (1, 0, 0, 0, whole),
-        (-1, 0, 0, 0, whole),
-        (1, 0, 0, 1, whole),
-        (-1, 0, 0, 1, whole),
-        (1, 0, -1, 0, first),
-        (-1, 0, 1, 0, last),
-        (1, 0, -1, 1, first),
-        (-1, 0, 1, 1, last),
-    )
+        [(0, 1, 0, 0, part) for part in parts]
+        + [(1, 0, 0, 0, whole), (-1, 0, 0, 0, whole)]
+        + [(1, 0, 0, 1, part) for part in parts]
+        + [(-1, 0, 0, 1, part) for part in parts]
+        + [(1, 0, -1, 0, first), (-1, 0, 1, 0, last)]
+        + [(1, 0, -1, 1, part) for part in parts[:2]]
+        + [(-1, 0, 1, 1, part) for part in parts[2:]]
+    )
+    follow = {4: (14,), 5: (15,), 6: (16,), 7: (17,), 12: (18,), 13: (19,)}
+    follow.update({p: (6 + p, 10 + p) for p in range(4)})
+    order = (0, 4, 5, 1, 6, 10, 14, 15, 2, 7, 11, 16, 3, 8, 12, 17, 9, 13, 18, 19)
 
     def hop(axis, n, landed):
         at, me, blocks, sent, arrived = (
@@ -245,22 +256,21 @@
             device_id_type=pl.DeviceIdType.MESH,
         )
 
-    for n in range(3):
+    for n in range(6):
         hop("row", n, False).start()
         hop("col", n, False).start()
     pass_on(0, False).start()
-    follow = {1: (5,), 2: (6,), 0: (3, 4), 3: (7,), 4: (8,)}
-    for n in (1, 2, 0, 3, 4, 5, 6, 7, 8):
+    for n in order:
         for axis in ("row", "col"):
             hop(axis, n, True).wait_recv()
             for later in follow.get(n, ()):
                 hop(axis, later, False).start()
         pass_on(n + 1, False).start()
-    for n in range(10):
+    for n in range(21):
         pass_on(n, True).wait_recv()
-    for n in range(10):
+    for n in range(21):
         pass_on(n, False).wait_send()
-    for n in range(9):
+    for n in range(20):
         hop("row", n, False).wait_send()
         hop("col", n, False).wait_send()
 
@@ -409,12 +419,12 @@
             pltpu.VMEM((ITERS, TD * row_count, TILE), F32),
             pltpu.SemaphoreType.DMA((4 * ITERS, large)),
             pltpu.SemaphoreType.DMA((4 * ITERS, large)),
-            pltpu.SemaphoreType.DMA((9,)),
-            pltpu.SemaphoreType.DMA((9,)),
-            pltpu.SemaphoreType.DMA((9,)),
-            pltpu.SemaphoreType.DMA((9,)),
-            pltpu.SemaphoreType.DMA((10,)),
-            pltpu.SemaphoreType.DMA((10,)),
+            pltpu.SemaphoreType.DMA((20,)),
+            pltpu.SemaphoreType.DMA((20,)),
+            pltpu.SemaphoreType.DMA((20,)),
+            pltpu.SemaphoreType.DMA((20,)),
+            pltpu.SemaphoreType.DMA((21,)),
+            pltpu.SemaphoreType.DMA((21,)),
         ],
         compiler_params=pltpu.CompilerParams(
             collective_id=0, has_side_effects=True, vmem_limit_bytes=48 * 2**20
@@ -447,7 +457,6 @@
     picks = picks.reshape(2, devices, per_dest).transpose(1, 0, 2).reshape(-1)
     outgoing = features.reshape(2 * rows_dev, width)[picks].reshape(devices, 2 * per_dest, width)
     ghost = lax.all_to_all(outgoing, ("row", "col"), 0, 0, tiled=True)
-    ghost = ghost.reshape(devices, 2, per_dest, width).transpose(1, 0, 2, 3).reshape(2, -1, width)
 
     embed = aggregate(features, ghost, adj_vals, blk_cols, blk_count, weight)
     embed = embed.reshape(2, TD, TILE, width)

time: 227 us -> 217 us (0.956)
  local copies, waits for them, and re-layouts: 17.3 us -> 11.3 us
  Pallas kernels: 177 us -> 173 us
    pallas_call x1, Pallas kernels: 152 us -> 147 us  [sinkhorn(): pl.pallas_call(sinkhorn_kernel, in_specs=[pl.BlockSpec(memory_space=pltpu...]
    unnamed x14 -> x12, local copies, waits for them, and re-layouts: 6.3 us -> 3.89 us
where the time goes in v5:
time: 217 us
  Pallas kernels  173 us (80%)
  waiting for transfers between devices  18.5 us (9%)
  local copies, waits for them, and re-layouts  11.3 us (5%)
  starting transfers between devices  11.1 us (5%)
    pallas_call x1, Pallas kernels, sinkhorn(): pl.pallas_call(sinkhorn_kernel, in_specs=[pl.BlockSpec(memory_space=pltpu...  147 us
    pallas_call x1, Pallas kernels, aggregate(): pl.pallas_call(aggregate_kernel, grid_spec=grid_spec, out_shape=jax.Shape...  26.3 us
    all_to_all x1, waiting for transfers between devices, on_device(): ghost = lax.all_to_all(outgoing, ('row', 'col'), 0, 0, tiled=True)  18.5 us
    all_to_all x1, starting transfers between devices, on_device(): ghost = lax.all_to_all(outgoing, ('row', 'col'), 0, 0, tiled=True)  11.1 us
    gather x1, local copies, waits for them, and re-layouts, on_device(): features.reshape(2 * rows_dev, width)[picks]  6.31 us
  transfers between devices with their start and end apart: 1, of which 1 were waited for; matrix products, arithmetic and copies ran while one was open for 0% of the time, Pallas kernels for 0%

profile of v5, /device:TPU:0, one launch (start us, length us, event | category | flops | bytes accessed | tf_op | source)
XLA Modules:
  0.0 216.6 jit_solution(10468851543448530400)
XLA Ops:
  0.6 0.7 reduce
  1.3 0.1 squeeze.9
  1.5 0.1 add_bitcast_fusion
  1.6 0.1 copy.12
  1.7 0.2 reshape.97
  1.9 0.0 copy-start.4
  1.9 0.0 copy-start.1
  1.9 0.0 copy-start.2
  2.0 0.0 copy-start.3
  2.0 6.3 %gather_fusion = f32[1024,256]{1,0:T(8,128)} fusion(f32[2048,256]{1,0:T(8,128)} %bitcast.22, s32[1024]{0:T(1024)S(1)} %broadcast_clamp_fusion), kind=kCustom, calls=%fused_computation | custom fusion | bytes 2101248 | tf_op jit(solution)/shard_map/gather | solution.py:458
  8.3 11.1 %all-to-all-start = ((f32[128,8,256]{2,1,0:T(8,128)}), f32[128,8,256]{2,1,0:T(8,128)S(1)}, u32[]{:S(2)}, u32[]{:S(2)}) async-start(f32[128,8,256]{2,1,0:T(8,128)} %bitcast.6), calls=%async_computation | async-start | bytes 2097152 | tf_op jit(solution)/shard_map/all_to_all | solution.py:459
  20.1 0.0 copy-done.4
  20.1 18.5 %all-to-all-done.ghost_ref = f32[128,8,256]{2,1,0:T(8,128)S(1)} async-done(((f32[128,8,256]{2,1,0:T(8,128)}), f32[128,8,256]{2,1,0:T(8,128)S(1)}, u32[]{:S(2)}, u32[]{:S(2)}) %all-to-all-start) | async-done | bytes 1048608 | tf_op jit(solution)/shard_map/all_to_all | solution.py:459
  38.6 0.0 copy-done.1
  38.6 0.0 copy-done.2
  38.6 0.0 copy-done.3
  38.6 26.3 %aggregate.1 = f32[2,1024,256]{2,1,0:T(8,128)} custom-call(s32[2,8,20]{2,1,0:T(8,128)S(1)} %copy-done.2, s32[2,8]{1,0:T(2,128)S(1)} %copy-done.3, bf16[2,8,20,128,128]{4,3,2,1,0:T(8,128)(2,1)} %adj_ref.1, f32[2,1024,256]{2,1,0:T(8,128)} %own_ref.1, f32[128,8,256]{2,1,0:T(8,128)S(1)} %all-to-all-done.ghost_ref, f32[256,256]{1,0:T(8,128)S(1)} %copy-done.1), custom_call_target="tpu_custom_call" | custom-call | flops 5368709120 | bytes 16777216 | tf_op jit(solution)/shard_map/aggregate/pallas_call | solution.py:100
  64.9 0.0 copy-start
  64.9 1.6 copy-done
  66.5 147.1 %sinkhorn.1 = (f32[48,128,128]{2,1,0:T(8,128)S(1)}, f32[128,128]{1,0:T(8,128)S(1)}, f32[64,128]{1,0:T(8,128)S(1)}) custom-call(s32[5,48]{1,0:T(8,128)S(1)} %stack.2.info, f32[2,8,128,256]{3,2,1,0:T(8,128)S(1)} %bitcast.20), custom_call_target="tpu_custom_call" | custom-call | tf_op jit(solution)/shard_map/sinkhorn/pallas_call | solution.py:402
  213.7 0.6 reshape.100
  214.3 1.7 copy.17
  216.0 0.6 copy.18
  (7 shorter events, 0.1 us)
Async XLA Ops:
  1.9 18.2 %copy-start.4 = (s32[1,1,2,48]{3,2,1,0:T(2,128)S(1)}, s32[1,1,2,48]{3,2,1,0:T(2,128)}, u32[]{:S(2)}) copy-start(s32[1,1,2,48]{3,2,1,0:T(2,128)} %param.14) | copy-start | bytes 1156
  1.9 36.7 %copy-start.1 = (f32[256,256]{1,0:T(8,128)S(1)}, f32[256,256]{1,0:T(8,128)}, u32[]{:S(2)}) copy-start(f32[256,256]{1,0:T(8,128)} %weight_ref.1) | copy-start | bytes 786436
  1.9 36.7 %copy-start.2 = (s32[2,8,20]{2,1,0:T(8,128)S(1)}, s32[2,8,20]{2,1,0:T(8,128)}, u32[]{:S(2)}) copy-start(s32[2,8,20]{2,1,0:T(8,128)} %cols.1) | copy-start | bytes 3844
  2.0 36.7 %copy-start.3 = (s32[2,8]{1,0:T(2,128)S(1)}, s32[2,8]{1,0:T(2,128)}, u32[]{:S(2)}) copy-start(s32[2,8]{1,0:T(2,128)} %count.1) | copy-start | bytes 196
  8.3 30.3 %all-to-all-start = ((f32[128,8,256]{2,1,0:T(8,128)}), f32[128,8,256]{2,1,0:T(8,128)S(1)}, u32[]{:S(2)}, u32[]{:S(2)}) async-start(f32[128,8,256]{2,1,0:T(8,128)} %bitcast.6), calls=%async_computation | async-start | bytes 2097152 | tf_op jit(solution)/shard_map/all_to_all | solution.py:459
  64.9 1.6 copy-start

commit v6 on v5

--- a/solution.py
+++ b/solution.py
@@ -55,20 +55,23 @@
     deg[...] = jnp.zeros_like(deg)
     n = count[g, t]
 
-    def pair(i, carry):
-        b = 2 * i
-        first = adj_ref[0, b]
-        second = adj_ref[0, b + 1]
-        second = jnp.where(b + 1 < n, second, jnp.zeros_like(second))
-        one = table[pl.ds(pl.multiple_of(cols[g, t, b] * TILE, TILE), TILE), :]
-        two = table[pl.ds(pl.multiple_of(cols[g, t, b + 1] * TILE, TILE), TILE), :]
-        left = jnp.concatenate([first, second], axis=1)
-        right = jnp.concatenate([one, two], axis=0)
+    def four(i, carry):
+        b = 4 * i
+        blocks = [adj_ref[0, b]]
+        for k in range(1, 4):
+            block = adj_ref[0, b + k]
+            blocks.append(jnp.where(b + k < n, block, jnp.zeros_like(block)))
+        rows = [
+            table[pl.ds(pl.multiple_of(cols[g, t, b + k] * TILE, TILE), TILE), :] for k in range(4)
+        ]
+        left = jnp.concatenate(blocks, axis=1)
+        right = jnp.concatenate(rows, axis=0)
         acc[...] += jnp.dot(left, right, preferred_element_type=F32)
-        deg[...] += first.astype(F32) + second.astype(F32)
+        one, two, three, last = [block.astype(F32) for block in blocks]
+        deg[...] += (one + two) + (three + last)
         return carry
 
-    lax.fori_loop(0, (n + 1) // 2, pair, 0)
+    lax.fori_loop(0, (n + 3) // 4, four, 0)
     summed = acc[:, :width] + acc[:, width:]
     degree = jnp.sum(deg[...], axis=1, keepdims=True)
     hi, lo = split_two(summed / jnp.sqrt(degree))
@@ -292,8 +295,7 @@
 
     def along_lanes(it):
         def eight(g, carry):
-            tops = jnp.zeros((TILE, TILE), F32)
-            sums = jnp.ones((TILE, TILE), F32)
+            found = jnp.ones((TILE, TILE), F32)
             for k in range(8):
                 s = 8 * g + k
                 x = plan[s]
@@ -301,9 +303,10 @@
                     x = x + col_all[it - 1, pl.ds(info[1, s], 1), :]
                 top = jnp.max(x, axis=1, keepdims=True)
                 total = jnp.sum(jnp.exp(x - top), axis=1, keepdims=True)
-                tops = jnp.where(lanes == k, top, tops)
-                sums = jnp.where(lanes == k, total, sums)
-            lse[pl.ds(8 * g, 8), :] = (jnp.transpose(tops) + jnp.log(jnp.transpose(sums)))[:8]
+                found = jnp.where(lanes == k, top, found)
+                found = jnp.where(lanes == k + 8, total, found)
+            found = jnp.transpose(found)
+            lse[pl.ds(8 * g, 8), :] = found[:8] + jnp.log(found[8:16])
             return carry
 
         lax.fori_loop(0, CAP // 8, eight, 0)

time: 217 us -> 210 us (0.968)
  Pallas kernels: 173 us -> 166 us
    pallas_call x1, Pallas kernels: 147 us -> 143 us  [sinkhorn(): pl.pallas_call(sinkhorn_kernel, in_specs=[pl.BlockSpec(memory_space=pltpu...]
    pallas_call x1, Pallas kernels: 26.3 us -> 23.3 us  [aggregate(): pl.pallas_call(aggregate_kernel, grid_spec=grid_spec, out_shape=jax.Shape...]
where the time goes in v6:
time: 210 us; the launch traced here: 209 us
  Pallas kernels  166 us (79%)
  waiting for transfers between devices  18.5 us (9%)
  local copies, waits for them, and re-layouts  11.3 us (5%)
  starting transfers between devices  11.1 us (5%)
    pallas_call x1, Pallas kernels, sinkhorn(): pl.pallas_call(sinkhorn_kernel, in_specs=[pl.BlockSpec(memory_space=pltpu...  143 us
    pallas_call x1, Pallas kernels, aggregate(): pl.pallas_call(aggregate_kernel, grid_spec=grid_spec, out_shape=jax.Shape...  23.3 us
    all_to_all x1, waiting for transfers between devices, on_device(): ghost = lax.all_to_all(outgoing, ('row', 'col'), 0, 0, tiled=True)  18.5 us
    all_to_all x1, starting transfers between devices, on_device(): ghost = lax.all_to_all(outgoing, ('row', 'col'), 0, 0, tiled=True)  11.1 us
    gather x1, local copies, waits for them, and re-layouts, on_device(): features.reshape(2 * rows_dev, width)[picks]  6.31 us
  transfers between devices with their start and end apart: 1, of which 1 were waited for; matrix products, arithmetic and copies ran while one was open for 0% of the time, Pallas kernels for 0%

profile of v6, /device:TPU:0, one launch (start us, length us, event | category | flops | bytes accessed | tf_op | source)
XLA Modules:
  0.0 209.1 jit_solution(12310167599968562795)
XLA Ops:
  0.6 0.7 reduce
  1.3 0.1 squeeze.9
  1.5 0.1 add_bitcast_fusion
  1.6 0.1 copy.12
  1.7 0.2 reshape.97
  1.9 0.0 copy-start.4
  1.9 0.0 copy-start.1
  1.9 0.0 copy-start.2
  2.0 0.0 copy-start.3
  2.0 6.3 %gather_fusion = f32[1024,256]{1,0:T(8,128)} fusion(f32[2048,256]{1,0:T(8,128)} %bitcast.22, s32[1024]{0:T(1024)S(1)} %broadcast_clamp_fusion), kind=kCustom, calls=%fused_computation | custom fusion | bytes 2101248 | tf_op jit(solution)/shard_map/gather | solution.py:461
  8.3 11.1 %all-to-all-start = ((f32[128,8,256]{2,1,0:T(8,128)}), f32[128,8,256]{2,1,0:T(8,128)S(1)}, u32[]{:S(2)}, u32[]{:S(2)}) async-start(f32[128,8,256]{2,1,0:T(8,128)} %bitcast.6), calls=%async_computation | async-start | bytes 2097152 | tf_op jit(solution)/shard_map/all_to_all | solution.py:462
  20.1 0.0 copy-done.4
  20.1 18.5 %all-to-all-done.ghost_ref = f32[128,8,256]{2,1,0:T(8,128)S(1)} async-done(((f32[128,8,256]{2,1,0:T(8,128)}), f32[128,8,256]{2,1,0:T(8,128)S(1)}, u32[]{:S(2)}, u32[]{:S(2)}) %all-to-all-start) | async-done | bytes 1048608 | tf_op jit(solution)/shard_map/all_to_all | solution.py:462
  38.6 0.0 copy-done.1
  38.6 0.0 copy-done.2
  38.6 0.0 copy-done.3
  38.6 23.3 %aggregate.1 = f32[2,1024,256]{2,1,0:T(8,128)} custom-call(s32[2,8,20]{2,1,0:T(8,128)S(1)} %copy-done.2, s32[2,8]{1,0:T(2,128)S(1)} %copy-done.3, bf16[2,8,20,128,128]{4,3,2,1,0:T(8,128)(2,1)} %adj_ref.1, f32[2,1024,256]{2,1,0:T(8,128)} %own_ref.1, f32[128,8,256]{2,1,0:T(8,128)S(1)} %all-to-all-done.ghost_ref, f32[256,256]{1,0:T(8,128)S(1)} %copy-done.1), custom_call_target="tpu_custom_call" | custom-call | flops 5368709120 | bytes 16777216 | tf_op jit(solution)/shard_map/aggregate/pallas_call | solution.py:103
  61.9 0.0 copy-start
  61.9 1.6 copy-done
  63.5 142.7 %sinkhorn.1 = (f32[48,128,128]{2,1,0:T(8,128)S(1)}, f32[128,128]{1,0:T(8,128)S(1)}, f32[64,128]{1,0:T(8,128)S(1)}) custom-call(s32[5,48]{1,0:T(8,128)S(1)} %stack.2.info, f32[2,8,128,256]{3,2,1,0:T(8,128)S(1)} %bitcast.20), custom_call_target="tpu_custom_call" | custom-call | tf_op jit(solution)/shard_map/sinkhorn/pallas_call | solution.py:405
  206.2 0.6 reshape.100
  206.9 1.7 copy.17
  208.5 0.6 copy.18
  (7 shorter events, 0.1 us)
Async XLA Ops:
  1.9 18.2 %copy-start.4 = (s32[1,1,2,48]{3,2,1,0:T(2,128)S(1)}, s32[1,1,2,48]{3,2,1,0:T(2,128)}, u32[]{:S(2)}) copy-start(s32[1,1,2,48]{3,2,1,0:T(2,128)} %param.14) | copy-start | bytes 1156
  1.9 36.7 %copy-start.1 = (f32[256,256]{1,0:T(8,128)S(1)}, f32[256,256]{1,0:T(8,128)}, u32[]{:S(2)}) copy-start(f32[256,256]{1,0:T(8,128)} %weight_ref.1) | copy-start | bytes 786436
  1.9 36.7 %copy-start.2 = (s32[2,8,20]{2,1,0:T(8,128)S(1)}, s32[2,8,20]{2,1,0:T(8,128)}, u32[]{:S(2)}) copy-start(s32[2,8,20]{2,1,0:T(8,128)} %cols.1) | copy-start | bytes 3844
  2.0 36.7 %copy-start.3 = (s32[2,8]{1,0:T(2,128)S(1)}, s32[2,8]{1,0:T(2,128)}, u32[]{:S(2)}) copy-start(s32[2,8]{1,0:T(2,128)} %count.1) | copy-start | bytes 196
  8.3 30.3 %all-to-all-start = ((f32[128,8,256]{2,1,0:T(8,128)}), f32[128,8,256]{2,1,0:T(8,128)S(1)}, u32[]{:S(2)}, u32[]{:S(2)}) async-start(f32[128,8,256]{2,1,0:T(8,128)} %bitcast.6), calls=%async_computation | async-start | bytes 2097152 | tf_op jit(solution)/shard_map/all_to_all | solution.py:462
  61.9 1.6 copy-start
